TPU v7x, 128 devices: a whole 4x4x4 slice. The times are simulated.
128 devices in a mesh: dp: 64 (over z, y, x), tensor: 2 (over core).
Axes of the slice: x: 4, y: 4, z: 4, core: 2. Of those that a mesh axis runs over, the one named last changes fastest.
Arguments:
- square_grad: float32 [32, 2359296], P(None, ('dp', 'tensor')), may hold values from -80 to 80
- square_state: float32 [32, 2359296], P(None, ('dp', 'tensor')), may hold values from -6 to 6
- swiglu_grad: float32 [24, 6291456], P(None, ('dp', 'tensor')), may hold values from -80 to 80
- swiglu_state: float32 [24, 6291456], P(None, ('dp', 'tensor')), may hold values from -6 to 6
- square_order: int32 [32], replicated, may hold values from 0 to 31, each once
- swiglu_order: int32 [24], replicated, may hold values from 0 to 23, each once
- owners: int32 [56], replicated, may hold values from 0 to 63, as said below
- vector_values: float32 [172032], P(('dp', 'tensor')), may hold values from -6 to 6
- vector_grad: float32 [172032], P(('dp', 'tensor')), may hold values from -6 to 6
- vector_first: float32 [172032], P(('dp', 'tensor')), may hold values from -4 to 4
- vector_second: float32 [172032], P(('dp', 'tensor')), may hold values from 0.01 to 1
- embed_values: float32 [8192, 1536], P('dp', 'tensor'), may hold values from -6 to 6
- embed_grad: float32 [8192, 1536], P('dp', 'tensor'), may hold values from -6 to 6
- embed_first: float32 [8192, 1536], P('dp', 'tensor'), may hold values from -4 to 4
- embed_second: float32 [8192, 1536], P('dp', 'tensor'), may hold values from 0.01 to 1
- embed_ranges: int32 [16, 2], replicated, may hold values from 0 to 8192, as said below
Outputs:
- square_next: float32 [32, 2359296], P(None, ('dp', 'tensor'))
- swiglu_next: float32 [24, 6291456], P(None, ('dp', 'tensor'))
- square_update: bfloat16 [32, 1536, 1536], P(None, 'dp', 'tensor')
- swiglu_update: bfloat16 [24, 1536, 4096], P(None, 'dp', 'tensor')
- owner_norms: float32 [64], P('dp')
- vector_step: float32 [172032], P(('dp', 'tensor'))
- first_vector: float32 [172032], P(('dp', 'tensor'))
- second_vector: float32 [172032], P(('dp', 'tensor'))
- embed_step: float32 [8192, 1536], P('dp', 'tensor')
- first_embed: float32 [8192, 1536], P('dp', 'tensor')
- second_embed: float32 [8192, 1536], P('dp', 'tensor')
Inputs may be any that keep to these rules, and one draw needn't show every extreme that they name: Different matrices have different owners. `square_order`: each matrix once. `swiglu_order`: each matrix once. `embed_ranges`: start < end in every row.
All inputs are finite; a program needn't handle non-finite values.
Results may differ from a plain program's by a relative error of at most 0.0065.
Values may be sent and summed in bfloat16 or wider, within the bound.
A program may use at most 128 MiB of HBM per device.

v0:
```python
import math

import jax
import jax.numpy as jnp
from jax import lax
from jax.sharding import PartitionSpec as P

D = 1536
FF = 4096
NS_STEPS = 2


QUINTIC_LINEAR = 3.4445
QUINTIC_CUBIC = -4.775
QUINTIC_FIFTH = 2.0315
MOMENTUM = 0.95
BIAS_FIRST = 1.0 - 0.9**10
BIAS_SECOND = 1.0 - 0.95**10


def momentum_terms(gradient, state):
    state_next = MOMENTUM * state + gradient
    return (state_next, (gradient + MOMENTUM * state_next).astype(jnp.bfloat16))


def adamw_terms(values, gradient, first, second):
    first_next = 0.9 * first + 0.1 * gradient
    second_next = 0.95 * second + 0.05 * gradient * gradient
    direction = (
        first_next / BIAS_FIRST / (jnp.sqrt(second_next / BIAS_SECOND) + 1e-08) + 0.1 * values
    )
    return (direction, first_next, second_next)


def table_lookup(table, positions):
    matches = positions[:, None] == jnp.arange(table.shape[0], dtype=jnp.int32)[None, :]
    return jnp.sum(jnp.where(matches, table[None, :], 0), axis=1)


def select_pieces(pieces, piece_owner, targets):
    matched = piece_owner[None, :] == targets[:, None]
    chosen = jnp.sum(
        jnp.where(matched, jnp.arange(piece_owner.shape[0], dtype=jnp.int32)[None, :], 0), axis=1
    )
    present = jnp.any(matched, axis=1)
    picked = jnp.where(present[:, None, None, None], pieces[chosen], jnp.zeros((), jnp.bfloat16))
    return (picked, chosen, present)


def local(
    square_grad,
    square_state,
    swiglu_grad,
    swiglu_state,
    square_order,
    swiglu_order,
    owners,
    vector_values,
    vector_grad,
    vector_first,
    vector_second,
    embed_values,
    embed_grad,
    embed_first,
    embed_second,
    embed_ranges,
):
    wide_count = lax.axis_size("dp")
    split_count = lax.axis_size("tensor")
    wide_index = lax.axis_index("dp")
    square_count = square_grad.shape[0]
    swiglu_count = swiglu_grad.shape[0]
    flat_rows = D // (wide_count * split_count)
    slot_width = FF // split_count
    square_width = D // split_count
    square_next, square_send = momentum_terms(square_grad, square_state)
    swiglu_next, swiglu_send = momentum_terms(swiglu_grad, swiglu_state)
    square_pieces = square_send.reshape(
        square_count, flat_rows, split_count, square_width
    ).transpose(0, 2, 1, 3)
    swiglu_pieces = swiglu_send.reshape(swiglu_count, flat_rows, split_count, slot_width).transpose(
        0, 2, 1, 3
    )
    square_owner = table_lookup(owners[:square_count], square_order)
    swiglu_owner = table_lookup(owners[square_count:], swiglu_order)
    targets = jnp.arange(wide_count, dtype=jnp.int32)
    square_mine = jnp.any(square_owner == wide_index)
    owned = square_mine | jnp.any(swiglu_owner == wide_index)
    factor = jnp.where(square_mine, jnp.float32(math.sqrt(D)), jnp.float32(math.sqrt(FF)))
    widened = jnp.pad(square_pieces, ((0, 0), (0, 0), (0, 0), (0, slot_width - square_width)))
    all_pieces = jnp.concatenate([widened, swiglu_pieces], axis=0)
    slot_owner = jnp.concatenate([square_owner, swiglu_owner])
    outgoing, chosen, present = select_pieces(all_pieces, slot_owner, targets)
    arrived = lax.all_to_all(
        outgoing.reshape(D, slot_width), ("dp", "tensor"), split_axis=0, concat_axis=0, tiled=True
    )
    iterate = arrived
    first_scale = jnp.float32(1.0)
    for round_index in range(NS_STEPS):
        current = iterate
        gram_part = lax.psum_scatter(
            jnp.einsum("rc,sc->rs", current, current, preferred_element_type=jnp.float32),
            "tensor",
            scatter_dimension=0,
            tiled=True,
        )
        if round_index == 0:
            squares_total = lax.psum(jnp.sum(gram_part * gram_part), "tensor")
            gram_scale = jnp.sqrt(squares_total) + 1e-06
            first_scale = gram_scale
        else:
            gram_scale = jnp.float32(1.0)
        normed_part = (gram_part / gram_scale).astype(jnp.bfloat16)
        squared = jnp.dot(
            normed_part,
            lax.all_gather(normed_part, "tensor", axis=0, tiled=True),
            preferred_element_type=jnp.float32,
        )
        polynomial = (
            QUINTIC_CUBIC * normed_part.astype(jnp.float32) + QUINTIC_FIFTH * squared
        ).astype(jnp.bfloat16)
        product = jnp.dot(
            lax.all_gather(polynomial, "tensor", axis=0, tiled=True),
            current,
            preferred_element_type=jnp.float32,
        )
        mixed = (QUINTIC_LINEAR * current.astype(jnp.float32) + product) / jnp.sqrt(gram_scale)
        if round_index == NS_STEPS - 1:
            iterate = (factor * mixed).astype(jnp.bfloat16)
        else:
            iterate = mixed.astype(jnp.bfloat16)
    returned = lax.all_to_all(
        iterate.reshape(wide_count, D // wide_count, slot_width),
        "dp",
        split_axis=0,
        concat_axis=0,
        tiled=True,
    )
    square_update = returned[owners[:square_count]][:, :, :square_width]
    swiglu_update = returned[owners[square_count:]]
    owner_norms = jnp.where(owned, 0.5 * jnp.log(first_scale), 0.0).reshape(1)
    vector_step, first_vector, second_vector = adamw_terms(
        vector_values, vector_grad, vector_first, vector_second
    )
    embed_rows = embed_values.shape[0]
    row_numbers = wide_index * embed_rows + jnp.arange(embed_rows, dtype=jnp.int32)
    inside = (row_numbers[:, None] >= embed_ranges[None, :, 0]) & (
        row_numbers[:, None] < embed_ranges[None, :, 1]
    )
    row_live = jnp.sum(inside.astype(jnp.int32), axis=1) > 0
    direction, first_next, second_next = adamw_terms(
        embed_values, embed_grad, embed_first, embed_second
    )
    embed_step = jnp.where(row_live[:, None], direction, 0.0)
    first_embed = jnp.where(row_live[:, None], first_next, embed_first)
    second_embed = jnp.where(row_live[:, None], second_next, embed_second)
    return (
        square_next,
        swiglu_next,
        square_update,
        swiglu_update,
        owner_norms,
        vector_step,
        first_vector,
        second_vector,
        embed_step,
        first_embed,
        second_embed,
    )


def solution(mesh):
    placed = (
        P(None, ("dp", "tensor")),
        P(None, ("dp", "tensor")),
        P(None, ("dp", "tensor")),
        P(None, ("dp", "tensor")),
        P(),
        P(),
        P(),
        P(("dp", "tensor")),
        P(("dp", "tensor")),
        P(("dp", "tensor")),
        P(("dp", "tensor")),
        P("dp", "tensor"),
        P("dp", "tensor"),
        P("dp", "tensor"),
        P("dp", "tensor"),
        P(),
    )
    return jax.shard_map(
        local,
        mesh=mesh,
        in_specs=placed,
        out_specs=(
            P(None, ("dp", "tensor")),
            P(None, ("dp", "tensor")),
            P(None, "dp", "tensor"),
            P(None, "dp", "tensor"),
            P("dp"),
            P(("dp", "tensor")),
            P(("dp", "tensor")),
            P(("dp", "tensor")),
            P("dp", "tensor"),
            P("dp", "tensor"),
            P("dp", "tensor"),
        ),
        check_vma=False,
    )
```

profile of v0, /device:TPU:4, one launch (start us, length us, event | category | flops | bytes accessed | tf_op | source)
XLA Modules:
  0.0 514.9 jit_solution(1465619128677415151)
XLA Ops:
  10.9 4.2 add_convert_fusion.3
  16.0 7.5 %add_convert_fusion.2 = (bf16[24,49152]{1,0:T(8,128)(2,1)}, f32[24,49152]{1,0:T(8,128)}) fusion(f32[24,49152]{1,0:T(8,128)} %param.18, f32[24,49152]{1,0:T(8,128)} %param.19), kind=kLoop, calls=%fused_computation.12 | loop fusion | flops 5898240 | bytes 16515072 | tf_op jit(solution)/shard_map/convert_element_type | solution.py:23
  23.5 3.5 reshape.75
  27.0 5.3 %fusion = bf16[56,2,12,2048]{3,1,2,0:T(2,128)(2,1)} fusion(bf16[32,2,12,768]{3,1,2,0:T(2,128)(2,1)S(1)} %bitcast.28, bf16[24,2,12,2048]{3,1,2,0:T(2,128)(2,1)S(1)} %bitcast.26), kind=kLoop, calls=%fused_computation.7 | loop fusion | flops 16515072 | bytes 9043968 | tf_op jit(solution)/shard_map/concatenate | solution.py:91
  32.3 17.6 %gather_fusion = bf16[64,2,12,2048]{3,1,2,0:T(2,128)(2,1)} fusion(bf16[56,2,12,2048]{3,1,2,0:T(2,128)(2,1)} %fusion, s32[1024]{0:T(1024)S(1)} %pad_clamp_fusion.2), kind=kCustom, calls=%fused_computation | custom fusion | bytes 12583168 | tf_op jit(solution)/shard_map/gather | solution.py:46
  49.9 9.4 %copy.29 = bf16[64,2,12,2048]{3,2,1,0:T(8,128)(2,1)} copy(bf16[64,2,12,2048]{3,1,2,0:T(2,128)(2,1)} %gather_fusion) | data formatting | bytes 12582912 | tf_op jit(solution)/shard_map/gather | solution.py:46
  59.5 7.2 %bitcast_select_fusion = bf16[128,12,2048]{2,1,0:T(8,128)(2,1)} fusion(bf16[64,2,12,2048]{3,2,1,0:T(8,128)(2,1)} %copy.29, pred[128]{0:T(512)(128)(4,1)S(1)} %broadcast_in_dim.100), kind=kLoop, calls=%fused_computation.6 | loop fusion | flops 3145728 | bytes 12583040 | tf_op jit(solution)/shard_map/jit(_where)/select_n | solution.py:46
  66.7 107.0 %all_to_all.14 = bf16[128,12,2048]{2,1,0:T(8,128)(2,1)} all-to-all(bf16[128,12,2048]{2,1,0:T(8,128)(2,1)} %bitcast_select_fusion), channel_id=1, replica_groups=mesh['dp'=64,'tensor'=2] {'dp','tensor'}, dimensions={0} | all-to-all | bytes 12582912 | tf_op jit(solution)/shard_map/all_to_all | solution.py:94
  173.8 10.7 %all_to_all.10 = bf16[1536,2048]{1,0:T(8,128)(2,1)} reshape(bf16[128,12,2048]{2,1,0:T(8,128)(2,1)} %all_to_all.14) | data formatting | bytes 12582912 | tf_op jit(solution)/shard_map/all_to_all | solution.py:94
  184.5 16.2 %fusion.8 = f32[1536,1536]{1,0:T(8,128)} fusion(bf16[1536,2048]{1,0:T(8,128)(2,1)} %all_to_all.10), kind=kOutput, calls=%fused_computation.48 | convolution fusion | flops 9663676416 | bytes 15728640 | tf_op jit(solution)/shard_map/rc,sc->rs/dot_general | solution.py:102
  200.8 18.6 %reduce-scatter.3.cloned.1.call-done = f32[768,1536]{1,0:T(8,128)} async-done(((f32[1536,1536]{1,0:T(8,128)}), f32[768,1536]{1,0:T(8,128)}) %reduce-scatter.3.cloned.1.call-update) | async-done | bytes 4718608 | tf_op jit(solution)/shard_map/reduce_scatter | solution.py:101
  219.4 4.2 multiply_reduce_fusion
  223.5 3.1 psum.7
  227.3 4.3 divide_convert_fusion.1
  231.7 18.6 %all-gather.5.cloned.1.call-done = bf16[1536,1536]{1,0:T(8,128)(2,1)} async-done(((bf16[768,1536]{1,0:T(8,128)(2,1)}), bf16[1536,1536]{1,0:T(8,128)(2,1)}) %all-gather.5.cloned.1.call-update) | async-done | bytes 4718608 | tf_op jit(solution)/shard_map/all_gather | solution.py:116
  250.3 9.1 %add_convert_fusion.1 = bf16[768,1536]{1,0:T(8,128)(2,1)} fusion(bf16[768,1536]{1,0:T(8,128)(2,1)} %divide_convert_fusion.1, bf16[1536,1536]{1,0:T(8,128)(2,1)} %all-gather.5.cloned.1.call-done), kind=kOutput, calls=%fused_computation.9 | convolution fusion | flops 3629776896 | bytes 9437184 | tf_op jit(solution)/shard_map/dot_general | solution.py:114
  259.7 18.4 %all-gather.7.cloned.1.call-done = bf16[1536,1536]{1,0:T(8,128)(2,1)} async-done(((bf16[768,1536]{1,0:T(8,128)(2,1)}), bf16[1536,1536]{1,0:T(8,128)(2,1)}) %all-gather.7.cloned.1.call-update) | async-done | bytes 4718608 | tf_op jit(solution)/shard_map/all_gather | solution.py:123
  278.1 14.9 %divide_convert_fusion = bf16[1536,2048]{1,0:T(8,128)(2,1)S(1)} fusion(bf16[1536,2048]{1,0:T(8,128)(2,1)} %all_to_all.10, bf16[1536,1536]{1,0:T(8,128)(2,1)} %all-gather.7.cloned.1.call-done, f32[]{:T(128)S(6)} %sqrt.13), kind=kOutput, calls=%fused_computation.5 | convolution fusion | flops 9679405056 | bytes 17301508 | tf_op jit(solution)/shard_map/dot_general | solution.py:122
  293.0 2.7 copy-done.13
  295.6 12.7 %fusion.9 = f32[1536,1536]{1,0:T(8,128)} fusion(bf16[1536,2048]{1,0:T(8,128)(2,1)S(1)} %divide_convert_fusion), kind=kOutput, calls=%fused_computation.49 | convolution fusion | flops 9663676416 | bytes 15728640 | tf_op jit(solution)/shard_map/rc,sc->rs/dot_general | solution.py:102
  308.4 22.0 %reduce-scatter.5.cloned.1.call-done = f32[768,1536]{1,0:T(8,128)} async-done(((f32[1536,1536]{1,0:T(8,128)}), f32[768,1536]{1,0:T(8,128)}) %reduce-scatter.5.cloned.1.call-update) | async-done | bytes 4718608 | tf_op jit(solution)/shard_map/reduce_scatter | solution.py:101
  330.4 4.0 convert_element_type.49
  334.7 18.5 %all-gather.9.cloned.1.call-done = bf16[1536,1536]{1,0:T(8,128)(2,1)} async-done(((bf16[768,1536]{1,0:T(8,128)(2,1)}), bf16[1536,1536]{1,0:T(8,128)(2,1)}) %all-gather.9.cloned.1.call-update) | async-done | bytes 4718608 | tf_op jit(solution)/shard_map/all_gather | solution.py:116
  353.2 9.1 %add_convert_fusion = bf16[768,1536]{1,0:T(8,128)(2,1)} fusion(bf16[768,1536]{1,0:T(8,128)(2,1)} %convert_element_type.49, bf16[1536,1536]{1,0:T(8,128)(2,1)} %all-gather.9.cloned.1.call-done), kind=kOutput, calls=%fused_computation.8 | convolution fusion | flops 3629776896 | bytes 9437184 | tf_op jit(solution)/shard_map/dot_general | solution.py:114
  363.6 17.4 %all-gather.11.cloned.1.call-done = bf16[1536,1536]{1,0:T(8,128)(2,1)} async-done(((bf16[768,1536]{1,0:T(8,128)(2,1)}), bf16[1536,1536]{1,0:T(8,128)(2,1)}) %all-gather.11.cloned.1.call-update) | async-done | bytes 4718608 | tf_op jit(solution)/shard_map/all_gather | solution.py:123
  380.9 16.6 %multiply_convert_fusion = bf16[1536,2048]{1,0:T(8,128)(2,1)} fusion(bf16[1536,2048]{1,0:T(8,128)(2,1)} %copy-done.13, bf16[1536,1536]{1,0:T(8,128)(2,1)} %all-gather.11.cloned.1.call-done, f32[]{:T(128)S(6)} %select_n.54), kind=kOutput, calls=%fused_computation.4 | convolution fusion | flops 9679405056 | bytes 17301508 | tf_op jit(solution)/shard_map/dot_general | solution.py:122
  397.6 10.7 %all-to-all-start.1 = ((bf16[64,24,2048]{2,1,0:T(8,128)(2,1)}), bf16[64,24,2048]{2,1,0:T(8,128)(2,1)}, u32[]{:S(2)}, u32[]{:S(2)}) async-start(bf16[64,24,2048]{2,1,0:T(8,128)(2,1)} %bitcast.27), calls=%async_computation.3 | async-start | bytes 12582912 | tf_op jit(solution)/shard_map/all_to_all | solution.py:132
  411.1 1.4 fusion.3
  412.6 84.5 %all-to-all-done.1 = bf16[64,24,2048]{2,1,0:T(8,128)(2,1)} async-done(((bf16[64,24,2048]{2,1,0:T(8,128)(2,1)}), bf16[64,24,2048]{2,1,0:T(8,128)(2,1)}, u32[]{:S(2)}, u32[]{:S(2)}) %all-to-all-start.1) | async-done | bytes 6291488 | tf_op jit(solution)/shard_map/all_to_all | solution.py:132
  497.1 3.5 gather_fusion.1
  500.7 1.1 slice.28
  501.8 5.0 gather_fusion.2
  (60 shorter events, 7.6 us)
Async XLA Ops:
  7.2 212.2 %reduce-scatter.3.cloned.1.call-start = ((), (), s32[]{:S(2)}) async-start(), calls=%async_computation.4 | async-start | bytes 14155776 | tf_op jit(solution)/shard_map/reduce_scatter | solution.py:101
  9.4 1.0 copy-start.9
  10.3 0.5 copy-start.11
  200.7 49.6 %all-gather.5.cloned.1.call-start = ((), (), s32[]{:S(2)}) async-start(), calls=%async_computation.5 | async-start | bytes 7077888 | tf_op jit(solution)/shard_map/all_gather | solution.py:116
  231.6 46.4 %all-gather.7.cloned.1.call-start = ((), (), s32[]{:S(2)}) async-start(), calls=%async_computation.6 | async-start | bytes 7077888 | tf_op jit(solution)/shard_map/all_gather | solution.py:123
  259.4 71.0 %reduce-scatter.5.cloned.1.call-start = ((), (), s32[]{:S(2)}) async-start(), calls=%async_computation.7 | async-start | bytes 14155776 | tf_op jit(solution)/shard_map/reduce_scatter | solution.py:101
  293.0 2.7 copy-start.13
  308.4 44.8 %all-gather.9.cloned.1.call-start = ((), (), s32[]{:S(2)}) async-start(), calls=%async_computation.8 | async-start | bytes 7077888 | tf_op jit(solution)/shard_map/all_gather | solution.py:116
  334.5 27.8 %copy-start.12 = (s32[32]{0:T(128)S(1)}, s32[32]{0:T(128)}, u32[]{:S(2)}) copy-start(s32[32]{0:T(128)} %copy-done.11) | copy-start | bytes 388
  334.5 46.5 %all-gather.11.cloned.1.call-start = ((), (), s32[]{:S(2)}) async-start(), calls=%async_computation.9 | async-start | bytes 7077888 | tf_op jit(solution)/shard_map/all_gather | solution.py:123
  397.5 10.8 %copy-start.10 = (s32[24]{0:T(128)S(1)}, s32[24]{0:T(128)}, u32[]{:S(2)}) copy-start(s32[24]{0:T(128)} %copy-done.9) | copy-start | bytes 292
  397.5 12.8 %copy-start.8 = (s32[16,2]{0,1:T(2,128)S(1)}, s32[16,2]{0,1:T(2,128)}, u32[]{:S(2)}) copy-start(s32[16,2]{0,1:T(2,128)} %param.31) | copy-start | bytes 388
  397.5 12.9 %copy-start.4 = (f32[1344]{0:T(1024)S(1)}, f32[1344]{0:T(1024)}, u32[]{:S(2)}) copy-start(f32[1344]{0:T(1024)} %param.23) | copy-start | bytes 16132
  397.6 12.9 %copy-start.5 = (f32[1344]{0:T(1024)S(1)}, f32[1344]{0:T(1024)}, u32[]{:S(2)}) copy-start(f32[1344]{0:T(1024)} %param.24) | copy-start | bytes 16132
  397.6 12.9 %copy-start.6 = (f32[1344]{0:T(1024)S(1)}, f32[1344]{0:T(1024)}, u32[]{:S(2)}) copy-start(f32[1344]{0:T(1024)} %param.25) | copy-start | bytes 16132
  397.6 12.9 %copy-start.7 = (f32[1344]{0:T(1024)S(1)}, f32[1344]{0:T(1024)}, u32[]{:S(2)}) copy-start(f32[1344]{0:T(1024)} %param.26) | copy-start | bytes 16132
  397.6 13.5 %copy-start = (f32[128,768]{1,0:T(8,128)S(1)}, f32[128,768]{1,0:T(8,128)}, u32[]{:S(2)}) copy-start(f32[128,768]{1,0:T(8,128)} %param.30) | copy-start | bytes 1179652
  397.6 13.5 %copy-start.1 = (f32[128,768]{1,0:T(8,128)S(1)}, f32[128,768]{1,0:T(8,128)}, u32[]{:S(2)}) copy-start(f32[128,768]{1,0:T(8,128)} %param.28) | copy-start | bytes 1179652
  397.6 13.5 %copy-start.2 = (f32[128,768]{1,0:T(8,128)S(1)}, f32[128,768]{1,0:T(8,128)}, u32[]{:S(2)}) copy-start(f32[128,768]{1,0:T(8,128)} %param.27) | copy-start | bytes 1179652
  397.6 13.5 %copy-start.3 = (f32[128,768]{1,0:T(8,128)S(1)}, f32[128,768]{1,0:T(8,128)}, u32[]{:S(2)}) copy-start(f32[128,768]{1,0:T(8,128)} %param.29) | copy-start | bytes 1179652
  397.6 99.5 %all-to-all-start.1 = ((bf16[64,24,2048]{2,1,0:T(8,128)(2,1)}), bf16[64,24,2048]{2,1,0:T(8,128)(2,1)}, u32[]{:S(2)}, u32[]{:S(2)}) async-start(bf16[64,24,2048]{2,1,0:T(8,128)(2,1)} %bitcast.27), calls=%async_computation.3 | async-start | bytes 12582912 | tf_op jit(solution)/shard_map/all_to_all | solution.py:132
Sparse Core Ops, SparseCore 0:
  200.8 18.4 reduce-scatter.2
  231.7 18.5 all-gather.4
  259.5 18.4 all-gather.6
  308.5 21.8 reduce-scatter.4
  334.6 18.5 all-gather.8
  362.4 18.4 all-gather.10
where the time goes:
time: 524 us; the launch traced here: 515 us
  waiting for transfers between devices  198 us (38%)
  blocking collectives  110 us (21%)
  matrix products  78.6 us (15%)
  local copies, waits for them, and re-layouts  55 us (10%)
  other arithmetic  43.4 us (8%)
  between operations  18.5 us (4%)
  starting transfers between devices  11.3 us (2%)
    all_to_all x1, blocking collectives, local(): lax.all_to_all(outgoing.reshape(D, slot_width), ('dp', 'tensor'), split_a...  107 us
    all_to_all x1, waiting for transfers between devices, local(): lax.all_to_all(iterate.reshape(wide_count, D // wide_count, slot_width),...  84.5 us
    reduce_scatter x2, waiting for transfers between devices, local(): lax.psum_scatter(jnp.einsum('rc,sc->rs', current, current, preferred_elem...  40.6 us
    all_gather x2, waiting for transfers between devices, local(): lax.all_gather(normed_part, 'tensor', axis=0, tiled=True)  37.1 us
    all_gather x2, waiting for transfers between devices, local(): lax.all_gather(polynomial, 'tensor', axis=0, tiled=True)  35.7 us
    dot_general x2, matrix products, local(): jnp.dot(lax.all_gather(polynomial, 'tensor', axis=0, tiled=True), current...  31.5 us
    dot_general x2, matrix products, local(): jnp.einsum('rc,sc->rs', current, current, preferred_element_type=jnp.floa...  29 us
    gather x2, local copies, waits for them, and re-layouts, select_pieces(): pieces[chosen]  27 us
  transfers between devices with their start and end apart: 7, of which 7 were waited for; matrix products, arithmetic and copies ran while one was open for 1% of the time, Pallas kernels for 0%

commit v1 on v0

v1 whole, which is shorter than its diff:
```python
import math

import jax
import jax.numpy as jnp
from jax import lax
from jax.experimental import pallas as pl
from jax.experimental.pallas import tpu as pltpu
from jax.sharding import PartitionSpec as P

D = 1536
FF = 4096
NS_STEPS = 2
MESH = pl.DeviceIdType.MESH

QUINTIC_LINEAR = 3.4445
QUINTIC_CUBIC = -4.775
QUINTIC_FIFTH = 2.0315
MOMENTUM = 0.95
BIAS_FIRST = 1.0 - 0.9**10
BIAS_SECOND = 1.0 - 0.95**10


def momentum_terms(gradient, state):
    state_next = MOMENTUM * state + gradient
    return (state_next, (gradient + MOMENTUM * state_next).astype(jnp.bfloat16))


def adamw_terms(values, gradient, first, second):
    first_next = 0.9 * first + 0.1 * gradient
    second_next = 0.95 * second + 0.05 * gradient * gradient
    direction = (
        first_next / BIAS_FIRST / (jnp.sqrt(second_next / BIAS_SECOND) + 1e-08) + 0.1 * values
    )
    return (direction, first_next, second_next)


def inverse_of(order):
    count = order.shape[0]
    return jnp.zeros((count,), jnp.int32).at[order].set(jnp.arange(count, dtype=jnp.int32))


def device_barrier(n_dev, me):
    barrier = pltpu.get_barrier_semaphore()

    def signal(k, carry):
        target = lax.rem(me + k, n_dev)
        pl.semaphore_signal(
            barrier, inc=1, device_id=(target // 2, lax.rem(target, 2)), device_id_type=MESH
        )
        return carry

    lax.fori_loop(1, n_dev, signal, 0)
    pl.semaphore_wait(barrier, n_dev - 1)


def scatter_kernel(n_sq, n_sw, sq_ref, sw_ref, out_ref, send_sem, recv_sem):
    d = lax.axis_index("dp")
    t = lax.axis_index("tensor")
    n_dev = lax.axis_size("dp") * 2
    me = d * 2 + t
    device_barrier(n_dev, me)

    def sq_copy(j):
        return pltpu.make_async_remote_copy(
            src_ref=sq_ref.at[j],
            dst_ref=out_ref.at[me, :, pl.ds(0, D)],
            send_sem=send_sem.at[j],
            recv_sem=recv_sem.at[0],
            device_id=(j, 0),
            device_id_type=MESH,
        )

    def sw_copy(j):
        return pltpu.make_async_remote_copy(
            src_ref=sw_ref.at[j],
            dst_ref=out_ref.at[me],
            send_sem=send_sem.at[n_sq + j],
            recv_sem=recv_sem.at[0],
            device_id=(n_sq + j, 0),
            device_id_type=MESH,
        )

    def start_sq(j, carry):
        @pl.when(me == 2 * j)
        def _():
            pltpu.make_async_copy(sq_ref.at[j], out_ref.at[me, :, pl.ds(0, D)], recv_sem.at[0]).start()

        @pl.when(me != 2 * j)
        def _():
            sq_copy(j).start()

        return carry

    def start_sw(j, carry):
        @pl.when(me == 2 * (n_sq + j))
        def _():
            pltpu.make_async_copy(sw_ref.at[j], out_ref.at[me], recv_sem.at[0]).start()

        @pl.when(me != 2 * (n_sq + j))
        def _():
            sw_copy(j).start()

        return carry

    lax.fori_loop(0, n_sq, start_sq, 0)
    lax.fori_loop(0, n_sw, start_sw, 0)

    @pl.when((t == 0) & (d < n_sq))
    def _():
        region = out_ref.at[:, :, pl.ds(0, D)]
        pltpu.make_async_copy(region, region, recv_sem.at[0]).wait()

    @pl.when((t == 0) & (d >= n_sq) & (d < n_sq + n_sw))
    def _():
        pltpu.make_async_copy(out_ref, out_ref, recv_sem.at[0]).wait()

    def wait_sq(j, carry):
        @pl.when(me != 2 * j)
        def _():
            sq_copy(j).wait_send()

        return carry

    def wait_sw(j, carry):
        @pl.when(me != 2 * (n_sq + j))
        def _():
            sw_copy(j).wait_send()

        return carry

    lax.fori_loop(0, n_sq, wait_sq, 0)
    lax.fori_loop(0, n_sw, wait_sw, 0)


def gather_kernel(n_sq, n_sw, it_ref, osq_ref, osw_ref, send_sem, recv_sem):
    d = lax.axis_index("dp")
    t = lax.axis_index("tensor")
    n_dev = lax.axis_size("dp") * 2
    me = d * 2 + t
    device_barrier(n_dev, me)
    is_sq = (t == 0) & (d < n_sq)
    is_sw = (t == 0) & (d >= n_sq) & (d < n_sq + n_sw)
    sq_w = osq_ref.shape[2]
    sw_w = osw_ref.shape[2]
    j_sq = jnp.minimum(d, n_sq - 1)
    j_sw = jnp.clip(d - n_sq, 0, n_sw - 1)

    def sq_copy(g):
        return pltpu.make_async_remote_copy(
            src_ref=it_ref.at[g // 2, :, pl.ds(pl.multiple_of(lax.rem(g, 2) * sq_w, 128), sq_w)],
            dst_ref=osq_ref.at[j_sq],
            send_sem=send_sem.at[g],
            recv_sem=recv_sem.at[0],
            device_id=(g // 2, lax.rem(g, 2)),
            device_id_type=MESH,
        )

    def sw_copy(g):
        return pltpu.make_async_remote_copy(
            src_ref=it_ref.at[g // 2, :, pl.ds(pl.multiple_of(lax.rem(g, 2) * sw_w, 128), sw_w)],
            dst_ref=osw_ref.at[j_sw],
            send_sem=send_sem.at[g],
            recv_sem=recv_sem.at[1],
            device_id=(g // 2, lax.rem(g, 2)),
            device_id_type=MESH,
        )

    @pl.when(is_sq)
    def _():
        def start(g, carry):
            @pl.when(g == me)
            def _():
                pltpu.make_async_copy(
                    it_ref.at[d, :, pl.ds(0, sq_w)], osq_ref.at[j_sq], recv_sem.at[0]
                ).start()

            @pl.when(g != me)
            def _():
                sq_copy(g).start()

            return carry

        lax.fori_loop(0, n_dev, start, 0)

    @pl.when(is_sw)
    def _():
        def start(g, carry):
            @pl.when(g == me)
            def _():
                pltpu.make_async_copy(
                    it_ref.at[d, :, pl.ds(0, sw_w)], osw_ref.at[j_sw], recv_sem.at[1]
                ).start()

            @pl.when(g != me)
            def _():
                sw_copy(g).start()

            return carry

        lax.fori_loop(0, n_dev, start, 0)

    pltpu.make_async_copy(osq_ref, osq_ref, recv_sem.at[0]).wait()
    pltpu.make_async_copy(osw_ref, osw_ref, recv_sem.at[1]).wait()

    @pl.when(is_sq)
    def _():
        def wait(g, carry):
            @pl.when(g != me)
            def _():
                sq_copy(g).wait_send()

            return carry

        lax.fori_loop(0, n_dev, wait, 0)

    @pl.when(is_sw)
    def _():
        def wait(g, carry):
            @pl.when(g != me)
            def _():
                sw_copy(g).wait_send()

            return carry

        lax.fori_loop(0, n_dev, wait, 0)


def orthogonalize(matrix, factor):
    iterate = matrix
    first_scale = jnp.float32(1.0)
    for round_index in range(NS_STEPS):
        gram = jnp.dot(iterate, iterate.T, preferred_element_type=jnp.float32)
        if round_index == 0:
            gram_scale = jnp.sqrt(jnp.sum(gram * gram)) + 1e-06
            first_scale = gram_scale
        else:
            gram_scale = jnp.float32(1.0)
        normed = (gram / gram_scale).astype(jnp.bfloat16)
        squared = jnp.dot(normed, normed, preferred_element_type=jnp.float32)
        polynomial = (QUINTIC_CUBIC * normed.astype(jnp.float32) + QUINTIC_FIFTH * squared).astype(
            jnp.bfloat16
        )
        product = jnp.dot(polynomial, iterate, preferred_element_type=jnp.float32)
        mixed = (QUINTIC_LINEAR * iterate.astype(jnp.float32) + product) / jnp.sqrt(gram_scale)
        if round_index == NS_STEPS - 1:
            iterate = (factor * mixed).astype(jnp.bfloat16)
        else:
            iterate = mixed.astype(jnp.bfloat16)
    return (iterate, first_scale)


def local(
    square_grad,
    square_state,
    swiglu_grad,
    swiglu_state,
    square_order,
    swiglu_order,
    owners,
    vector_values,
    vector_grad,
    vector_first,
    vector_second,
    embed_values,
    embed_grad,
    embed_first,
    embed_second,
    embed_ranges,
):
    wide_count = lax.axis_size("dp")
    n_dev = wide_count * 2
    d = lax.axis_index("dp")
    t = lax.axis_index("tensor")
    n_sq = square_grad.shape[0]
    n_sw = swiglu_grad.shape[0]
    flat_rows = D // n_dev
    out_rows = D // wide_count
    square_next, square_send = momentum_terms(square_grad, square_state)
    swiglu_next, swiglu_send = momentum_terms(swiglu_grad, swiglu_state)
    sq_pieces = square_send.reshape(n_sq, flat_rows, D)
    sw_pieces = swiglu_send.reshape(n_sw, flat_rows, FF)

    arrived = pl.pallas_call(
        lambda *refs: scatter_kernel(n_sq, n_sw, *refs),
        out_shape=jax.ShapeDtypeStruct((n_dev, flat_rows, FF), jnp.bfloat16),
        in_specs=[pl.BlockSpec(memory_space=pl.ANY)] * 2,
        out_specs=pl.BlockSpec(memory_space=pl.ANY),
        scratch_shapes=[
            pltpu.SemaphoreType.DMA((n_sq + n_sw,)),
            pltpu.SemaphoreType.DMA((1,)),
        ],
        compiler_params=pltpu.CompilerParams(collective_id=0, has_side_effects=True),
    )(sq_pieces, sw_pieces)

    is_sq = (t == 0) & (d < n_sq)
    is_sw = (t == 0) & (d >= n_sq) & (d < n_sq + n_sw)
    width = jnp.where(is_sq, D, jnp.where(is_sw, FF, 0))
    columns = lax.broadcasted_iota(jnp.int32, (D, FF), 1)
    matrix = jnp.where(columns < width, arrived.reshape(D, FF), jnp.zeros((), jnp.bfloat16))
    factor = jnp.where(is_sq, jnp.float32(math.sqrt(D)), jnp.float32(math.sqrt(FF)))
    iterate, first_scale = orthogonalize(matrix, factor)

    returned_sq, returned_sw = pl.pallas_call(
        lambda *refs: gather_kernel(n_sq, n_sw, *refs),
        out_shape=(
            jax.ShapeDtypeStruct((n_sq, out_rows, D // 2), jnp.bfloat16),
            jax.ShapeDtypeStruct((n_sw, out_rows, FF // 2), jnp.bfloat16),
        ),
        in_specs=[pl.BlockSpec(memory_space=pl.ANY)],
        out_specs=(pl.BlockSpec(memory_space=pl.ANY), pl.BlockSpec(memory_space=pl.ANY)),
        scratch_shapes=[
            pltpu.SemaphoreType.DMA((n_dev,)),
            pltpu.SemaphoreType.DMA((2,)),
        ],
        compiler_params=pltpu.CompilerParams(collective_id=1, has_side_effects=True),
    )(iterate.reshape(wide_count, out_rows, FF))

    inv_sq = inverse_of(square_order)
    inv_sw = inverse_of(swiglu_order)
    square_update = returned_sq[inv_sq]
    swiglu_update = returned_sw[inv_sw]

    slots = jnp.arange(n_sq + n_sw, dtype=jnp.int32)
    mine = (is_sq | is_sw) & (slots == d)
    slot_norms = lax.psum(jnp.where(mine, 0.5 * jnp.log(first_scale), 0.0), ("dp", "tensor"))
    matrix_slot = jnp.concatenate([inv_sq, n_sq + inv_sw])
    matrix_norms = slot_norms[matrix_slot]
    owner_norms = jnp.sum(jnp.where(owners == d, matrix_norms, 0.0)).reshape(1)

    vector_step, first_vector, second_vector = adamw_terms(
        vector_values, vector_grad, vector_first, vector_second
    )
    embed_rows = embed_values.shape[0]
    row_numbers = d * embed_rows + jnp.arange(embed_rows, dtype=jnp.int32)
    inside = (row_numbers[:, None] >= embed_ranges[None, :, 0]) & (
        row_numbers[:, None] < embed_ranges[None, :, 1]
    )
    row_live = jnp.sum(inside.astype(jnp.int32), axis=1) > 0
    direction, first_next, second_next = adamw_terms(
        embed_values, embed_grad, embed_first, embed_second
    )
    embed_step = jnp.where(row_live[:, None], direction, 0.0)
    first_embed = jnp.where(row_live[:, None], first_next, embed_first)
    second_embed = jnp.where(row_live[:, None], second_next, embed_second)
    return (
        square_next,
        swiglu_next,
        square_update,
        swiglu_update,
        owner_norms,
        vector_step,
        first_vector,
        second_vector,
        embed_step,
        first_embed,
        second_embed,
    )


def solution(mesh):
    placed = (
        P(None, ("dp", "tensor")),
        P(None, ("dp", "tensor")),
        P(None, ("dp", "tensor")),
        P(None, ("dp", "tensor")),
        P(),
        P(),
        P(),
        P(("dp", "tensor")),
        P(("dp", "tensor")),
        P(("dp", "tensor")),
        P(("dp", "tensor")),
        P("dp", "tensor"),
        P("dp", "tensor"),
        P("dp", "tensor"),
        P("dp", "tensor"),
        P(),
    )
    return jax.shard_map(
        local,
        mesh=mesh,
        in_specs=placed,
        out_specs=(
            P(None, ("dp", "tensor")),
            P(None, ("dp", "tensor")),
            P(None, "dp", "tensor"),
            P(None, "dp", "tensor"),
            P("dp"),
            P(("dp", "tensor")),
            P(("dp", "tensor")),
            P(("dp", "tensor")),
            P("dp", "tensor"),
            P("dp", "tensor"),
            P("dp", "tensor"),
        ),
        check_vma=False,
    )
```

time: 524 us -> 585 us (1.12)
  the two profiles are of different devices: /device:TPU:4 before, /device:TPU:121 now
where the time goes in v1:
time: 585 us; the launch traced here: 584 us
  Pallas kernels  240 us (41%)
  matrix products  141 us (24%)
  blocking collectives  118 us (20%)
  local copies, waits for them, and re-layouts  51.2 us (9%)
  other arithmetic  32.8 us (6%)
    pallas_call x1, Pallas kernels, local(): pl.pallas_call(lambda *refs: gather_kernel(n_sq, n_sw, *refs), out_shape=...  136 us
    psum x1, blocking collectives, local(): lax.psum(jnp.where(mine, 0.5 * jnp.log(first_scale), 0.0), ('dp', 'tensor'))  118 us
    pallas_call x1, Pallas kernels, local(): pl.pallas_call(lambda *refs: scatter_kernel(n_sq, n_sw, *refs), out_shape...  104 us
    dot_general x2, matrix products, orthogonalize(): product = jnp.dot(polynomial, iterate, preferred_element_type=jnp.float32)  58.4 us
    dot_general x2, matrix products, orthogonalize(): gram = jnp.dot(iterate, iterate.T, preferred_element_type=jnp.float32)  57.3 us
    dot_general x2, matrix products, orthogonalize(): squared = jnp.dot(normed, normed, preferred_element_type=jnp.float32)  25.1 us
    reshape x1, local copies, waits for them, and re-layouts, local(): arrived.reshape(D, FF)  18.2 us
    select_n x1, local copies, waits for them, and re-layouts, local(): jnp.where(columns < width, arrived.reshape(D, FF), jnp.zeros((), jnp.bflo...  18.1 us

profile of v1, /device:TPU:121, one launch (start us, length us, event | category | flops | bytes accessed | tf_op | source)
XLA Modules:
  0.0 583.7 jit_solution(4407186353374141654)
XLA Ops:
  0.7 0.7 compare_select_fusion.4
  1.3 0.7 compare_select_fusion.2
  2.0 0.6 scatter_custom_fusion.1
  2.7 0.7 scatter_custom_fusion
  3.4 0.1 fusion.9
  3.5 0.8 slice_bitcast_fusion.1
  4.2 0.1 convert_reduce_fusion
  4.3 0.6 pad_clamp_fusion
  4.9 0.6 pad_clamp_fusion.2
  5.5 0.6 pad_clamp_fusion.1
  6.1 1.4 multiply_add_fusion.3
  7.5 2.8 fusion.6
  10.2 4.2 add_convert_fusion.3
  14.4 1.8 reshape.139.refs_0_
  16.2 6.7 %add_convert_fusion.2 = (bf16[24,49152]{1,0:T(8,128)(2,1)S(1)}, f32[24,49152]{1,0:T(8,128)}) fusion(f32[24,49152]{1,0:T(8,128)} %param.18, f32[24,49152]{1,0:T(8,128)} %param.19), kind=kLoop, calls=%fused_computation.19 | loop fusion | flops 5898240 | bytes 16515072 | tf_op jit(solution)/shard_map/convert_element_type | solution.py:25
  22.9 3.3 reshape.140.refs_1_
  26.2 104.0 %shard_map.239 = bf16[128,12,4096]{2,1,0:T(8,128)(2,1)} custom-call(bf16[32,12,1536]{2,1,0:T(8,128)(2,1)} %reshape.139.refs_0_, bf16[24,12,4096]{2,1,0:T(8,128)(2,1)} %reshape.140.refs_1_), custom_call_target="tpu_custom_call" | custom-call | tf_op jit(solution)/shard_map/pallas_call | solution.py:283
  130.1 18.2 %reshape.141 = bf16[1536,4096]{1,0:T(8,128)(2,1)} reshape(bf16[128,12,4096]{2,1,0:T(8,128)(2,1)} %shard_map.239) | data formatting | bytes 25165824 | tf_op jit(solution)/shard_map/reshape | solution.py:299
  148.3 13.8 %broadcast_select_fusion = bf16[128,12,4096]{2,1,0:T(8,128)(2,1)} fusion(bf16[128,12,4096]{2,1,0:T(8,128)(2,1)} %shard_map.239, pred[4096]{0:T(1024)(128)(4,1)S(1)} %iota_compare_fusion), kind=kLoop, calls=%fused_computation.7 | loop fusion | flops 6291456 | bytes 25169920 | tf_op jit(solution)/shard_map/jit(_where)/select_n | solution.py:299
  162.2 18.1 %select_n.68 = bf16[1536,4096]{1,0:T(8,128)(2,1)} reshape(bf16[128,12,4096]{2,1,0:T(8,128)(2,1)} %broadcast_select_fusion) | data formatting | bytes 25165824 | tf_op jit(solution)/shard_map/jit(_where)/select_n | solution.py:299
  180.2 30.3 %multiply_reduce_fusion = (f32[]{:T(128)}, f32[1536,1536]{1,0:T(8,128)}) fusion(bf16[1536,4096]{1,0:T(8,128)(2,1)} %select_n.68), kind=kOutput, calls=%fused_computation.15 | convolution fusion | flops 19332071424 | bytes 22020100 | tf_op jit(solution)/shard_map/dot_general | solution.py:232
  211.4 16.8 %add_convert_fusion.1.clone.5 = bf16[1536,1536]{1,0:T(8,128)(2,1)} fusion(f32[1536,1536]{1,0:T(8,128)} %get-tuple-element.30, f32[]{:T(128)S(6)} %add.101), kind=kOutput, calls=%fused_computation.13.clone.clone.clone.2 | convolution fusion | flops 7268990976 | bytes 14155780 | tf_op jit(solution)/shard_map/dot_general | solution.py:239
  228.2 30.4 %divide_convert_fusion = bf16[1536,4096]{1,0:T(8,128)(2,1)} fusion(f32[]{:T(128)S(6)} %sqrt.13, bf16[1536,4096]{1,0:T(8,128)(2,1)} %reshape.141, pred[4096]{0:T(1024)(128)(4,1)S(1)} %iota_compare_fusion, bf16[1536,1536]{1,0:T(8,128)(2,1)} %add_convert_fusion.1.clone.5), kind=kOutput, calls=%fused_computation.6 | convolution fusion | flops 19371393024 | bytes 29888516 | tf_op jit(solution)/shard_map/dot_general | solution.py:243
  258.6 117.6 %psum.7 = f32[56]{0:T(128)S(1)} all-reduce(f32[56]{0:T(128)S(1)} %and_select_fusion), channel_id=1, replica_groups=mesh['dp'=64,'tensor'=2] {'dp','tensor'}, use_global_device_ids=true, to_apply=%region_3.4 | all-reduce | flops 56 | bytes 448 | tf_op jit(solution)/shard_map/psum | solution.py:325
  376.1 0.9 gather_fusion.2
  377.0 0.6 fusion.8
  377.7 27.0 %convolution_convert_fusion = bf16[1536,1536]{1,0:T(8,128)(2,1)S(1)} fusion(bf16[1536,4096]{1,0:T(8,128)(2,1)} %divide_convert_fusion), kind=kOutput, calls=%fused_computation.16 | convolution fusion | flops 19329712128 | bytes 17301504 | tf_op jit(solution)/shard_map/dot_general | solution.py:232
  404.7 8.2 %add_convert_fusion.clone.4 = bf16[1536,1536]{1,0:T(8,128)(2,1)S(1)} fusion(bf16[1536,1536]{1,0:T(8,128)(2,1)S(1)} %convolution_convert_fusion), kind=kOutput, calls=%fused_computation.12.clone.clone.clone.1 | convolution fusion | flops 7259553792 | bytes 9437184 | tf_op jit(solution)/shard_map/dot_general | solution.py:239
  412.9 28.0 %multiply_convert_fusion = bf16[1536,4096]{1,0:T(8,128)(2,1)} fusion(bf16[1536,4096]{1,0:T(8,128)(2,1)} %divide_convert_fusion, f32[]{:T(128)S(6)} %select_n.63, bf16[1536,1536]{1,0:T(8,128)(2,1)S(1)} %add_convert_fusion.clone.4), kind=kOutput, calls=%fused_computation.5 | convolution fusion | flops 19358810112 | bytes 29884420 | tf_op jit(solution)/shard_map/dot_general | solution.py:243
  441.0 135.7 %shard_map.240 = (bf16[32,24,768]{2,1,0:T(8,128)(2,1)}, bf16[24,24,2048]{2,1,0:T(8,128)(2,1)}) custom-call(bf16[64,24,4096]{2,1,0:T(8,128)(2,1)} %bitcast.29), custom_call_target="tpu_custom_call" | custom-call | tf_op jit(solution)/shard_map/pallas_call | solution.py:303
  576.7 3.0 gather_fusion
  579.7 4.0 gather_fusion.1
  (10 shorter events, 0.0 us)
Async XLA Ops:
  228.2 148.9 %copy-start = (s32[56]{0:T(128)S(1)}, s32[56]{0:T(128)}, u32[]{:S(2)}) copy-start(s32[56]{0:T(128)} %param.22) | copy-start | bytes 676

commit v2 on v1

v2 whole, which is shorter than its diff:
```python
import math

import jax
import jax.numpy as jnp
from jax import lax
from jax.experimental import pallas as pl
from jax.experimental.pallas import tpu as pltpu
from jax.sharding import PartitionSpec as P

D = 1536
FF = 4096
NS_STEPS = 2
MESH = pl.DeviceIdType.MESH

QUINTIC_LINEAR = 3.4445
QUINTIC_CUBIC = -4.775
QUINTIC_FIFTH = 2.0315
MOMENTUM = 0.95
BIAS_FIRST = 1.0 - 0.9**10
BIAS_SECOND = 1.0 - 0.95**10


def momentum_terms(gradient, state):
    state_next = MOMENTUM * state + gradient
    return (state_next, (gradient + MOMENTUM * state_next).astype(jnp.bfloat16))


def adamw_terms(values, gradient, first, second):
    first_next = 0.9 * first + 0.1 * gradient
    second_next = 0.95 * second + 0.05 * gradient * gradient
    direction = (
        first_next / BIAS_FIRST / (jnp.sqrt(second_next / BIAS_SECOND) + 1e-08) + 0.1 * values
    )
    return (direction, first_next, second_next)


def inverse_of(order):
    count = order.shape[0]
    return jnp.zeros((count,), jnp.int32).at[order].set(jnp.arange(count, dtype=jnp.int32))


def device_barrier(n_dev, me, pairs):
    barrier = pltpu.get_barrier_semaphore()
    t = lax.axis_index("tensor")

    def signal(k, carry):
        target = lax.rem(me + k, n_dev)
        if pairs:
            device = (target // 2, lax.rem(target, 2))
        else:
            device = (target, t)
        pl.semaphore_signal(barrier, inc=1, device_id=device, device_id_type=MESH)
        return carry

    lax.fori_loop(1, n_dev, signal, 0)
    pl.semaphore_wait(barrier, n_dev - 1)


def scatter_kernel(n_sq, n_sw, sq_ref, sw_ref, zero_ref, out_ref, send_sem, recv_sem):
    del zero_ref
    d = lax.axis_index("dp")
    t = lax.axis_index("tensor")
    n_dev = lax.axis_size("dp") * 2
    me = d * 2 + t
    n_pairs = 2 * (n_sq + n_sw)
    sq_w = sq_ref.shape[2] // 2
    sw_w = sw_ref.shape[2] // 2
    device_barrier(n_dev, me, True)

    def sq_copy(g, h):
        return pltpu.make_async_remote_copy(
            src_ref=sq_ref.at[g, :, pl.ds(pl.multiple_of(h * sq_w, 128), sq_w)],
            dst_ref=out_ref.at[me, :, pl.ds(0, sq_w)],
            send_sem=send_sem.at[2 * g + h],
            recv_sem=recv_sem.at[0],
            device_id=(g, h),
            device_id_type=MESH,
        )

    def sw_copy(g, h):
        j = g - n_sq
        return pltpu.make_async_remote_copy(
            src_ref=sw_ref.at[j, :, pl.ds(pl.multiple_of(h * sw_w, 128), sw_w)],
            dst_ref=out_ref.at[me, :, pl.ds(0, sw_w)],
            send_sem=send_sem.at[2 * g + h],
            recv_sem=recv_sem.at[0],
            device_id=(g, h),
            device_id_type=MESH,
        )

    def start(k, carry):
        q = lax.rem(k + me, n_pairs)
        g = q // 2
        h = lax.rem(q, 2)
        local = (g == d) & (h == t)

        @pl.when(local & (g < n_sq))
        def _():
            pltpu.make_async_copy(
                sq_ref.at[g, :, pl.ds(pl.multiple_of(h * sq_w, 128), sq_w)],
                out_ref.at[me, :, pl.ds(0, sq_w)],
                recv_sem.at[0],
            ).start()

        @pl.when(local & (g >= n_sq))
        def _():
            pltpu.make_async_copy(
                sw_ref.at[g - n_sq, :, pl.ds(pl.multiple_of(h * sw_w, 128), sw_w)],
                out_ref.at[me, :, pl.ds(0, sw_w)],
                recv_sem.at[0],
            ).start()

        @pl.when(jnp.logical_not(local) & (g < n_sq))
        def _():
            sq_copy(g, h).start()

        @pl.when(jnp.logical_not(local) & (g >= n_sq))
        def _():
            sw_copy(g, h).start()

        return carry

    lax.fori_loop(0, n_pairs, start, 0)

    @pl.when(d < n_sq)
    def _():
        region = out_ref.at[:, :, pl.ds(0, sq_w)]
        pltpu.make_async_copy(region, region, recv_sem.at[0]).wait()

    @pl.when((d >= n_sq) & (d < n_sq + n_sw))
    def _():
        region = out_ref.at[:, :, pl.ds(0, sw_w)]
        pltpu.make_async_copy(region, region, recv_sem.at[0]).wait()

    def wait(q, carry):
        g = q // 2
        h = lax.rem(q, 2)
        local = (g == d) & (h == t)

        @pl.when(jnp.logical_not(local) & (g < n_sq))
        def _():
            sq_copy(g, h).wait_send()

        @pl.when(jnp.logical_not(local) & (g >= n_sq))
        def _():
            sw_copy(g, h).wait_send()

        return carry

    lax.fori_loop(0, n_pairs, wait, 0)


def gather_kernel(n_sq, n_sw, it_ref, osq_ref, osw_ref, send_sem, recv_sem):
    d = lax.axis_index("dp")
    t = lax.axis_index("tensor")
    n_dp = lax.axis_size("dp")
    device_barrier(n_dp, d, False)
    is_sq = d < n_sq
    is_sw = (d >= n_sq) & (d < n_sq + n_sw)
    sq_w = osq_ref.shape[2]
    sw_w = osw_ref.shape[2]
    j_sq = jnp.minimum(d, n_sq - 1)
    j_sw = jnp.clip(d - n_sq, 0, n_sw - 1)

    def sq_copy(r):
        return pltpu.make_async_remote_copy(
            src_ref=it_ref.at[r, :, pl.ds(0, sq_w)],
            dst_ref=osq_ref.at[j_sq],
            send_sem=send_sem.at[r],
            recv_sem=recv_sem.at[0],
            device_id=(r, t),
            device_id_type=MESH,
        )

    def sw_copy(r):
        return pltpu.make_async_remote_copy(
            src_ref=it_ref.at[r, :, pl.ds(0, sw_w)],
            dst_ref=osw_ref.at[j_sw],
            send_sem=send_sem.at[r],
            recv_sem=recv_sem.at[1],
            device_id=(r, t),
            device_id_type=MESH,
        )

    @pl.when(is_sq)
    def _():
        def start(k, carry):
            r = lax.rem(d + k, n_dp)

            @pl.when(r == d)
            def _():
                pltpu.make_async_copy(
                    it_ref.at[d, :, pl.ds(0, sq_w)], osq_ref.at[j_sq], recv_sem.at[0]
                ).start()

            @pl.when(r != d)
            def _():
                sq_copy(r).start()

            return carry

        lax.fori_loop(0, n_dp, start, 0)

    @pl.when(is_sw)
    def _():
        def start(k, carry):
            r = lax.rem(d + k, n_dp)

            @pl.when(r == d)
            def _():
                pltpu.make_async_copy(
                    it_ref.at[d, :, pl.ds(0, sw_w)], osw_ref.at[j_sw], recv_sem.at[1]
                ).start()

            @pl.when(r != d)
            def _():
                sw_copy(r).start()

            return carry

        lax.fori_loop(0, n_dp, start, 0)

    pltpu.make_async_copy(osq_ref, osq_ref, recv_sem.at[0]).wait()
    pltpu.make_async_copy(osw_ref, osw_ref, recv_sem.at[1]).wait()

    @pl.when(is_sq)
    def _():
        def wait(r, carry):
            @pl.when(r != d)
            def _():
                sq_copy(r).wait_send()

            return carry

        lax.fori_loop(0, n_dp, wait, 0)

    @pl.when(is_sw)
    def _():
        def wait(r, carry):
            @pl.when(r != d)
            def _():
                sw_copy(r).wait_send()

            return carry

        lax.fori_loop(0, n_dp, wait, 0)


def orthogonalize(arrived, factor):
    iterate = arrived
    first_scale = jnp.float32(1.0)
    for round_index in range(NS_STEPS):
        current = iterate
        gram_part = lax.psum_scatter(
            jnp.einsum("rc,sc->rs", current, current, preferred_element_type=jnp.float32),
            "tensor",
            scatter_dimension=0,
            tiled=True,
        )
        if round_index == 0:
            squares_total = lax.psum(jnp.sum(gram_part * gram_part), "tensor")
            gram_scale = jnp.sqrt(squares_total) + 1e-06
            first_scale = gram_scale
        else:
            gram_scale = jnp.float32(1.0)
        normed_part = (gram_part / gram_scale).astype(jnp.bfloat16)
        squared = jnp.dot(
            normed_part,
            lax.all_gather(normed_part, "tensor", axis=0, tiled=True),
            preferred_element_type=jnp.float32,
        )
        polynomial = (
            QUINTIC_CUBIC * normed_part.astype(jnp.float32) + QUINTIC_FIFTH * squared
        ).astype(jnp.bfloat16)
        product = jnp.dot(
            lax.all_gather(polynomial, "tensor", axis=0, tiled=True),
            current,
            preferred_element_type=jnp.float32,
        )
        mixed = (QUINTIC_LINEAR * current.astype(jnp.float32) + product) / jnp.sqrt(gram_scale)
        if round_index == NS_STEPS - 1:
            iterate = (factor * mixed).astype(jnp.bfloat16)
        else:
            iterate = mixed.astype(jnp.bfloat16)
    return (iterate, first_scale)


def local(
    square_grad,
    square_state,
    swiglu_grad,
    swiglu_state,
    square_order,
    swiglu_order,
    owners,
    vector_values,
    vector_grad,
    vector_first,
    vector_second,
    embed_values,
    embed_grad,
    embed_first,
    embed_second,
    embed_ranges,
):
    wide_count = lax.axis_size("dp")
    n_dev = wide_count * 2
    d = lax.axis_index("dp")
    t = lax.axis_index("tensor")
    n_sq = square_grad.shape[0]
    n_sw = swiglu_grad.shape[0]
    flat_rows = D // n_dev
    out_rows = D // wide_count
    square_next, square_send = momentum_terms(square_grad, square_state)
    swiglu_next, swiglu_send = momentum_terms(swiglu_grad, swiglu_state)
    sq_pieces = square_send.reshape(n_sq, flat_rows, D)
    sw_pieces = swiglu_send.reshape(n_sw, flat_rows, FF)

    half = FF // 2
    arrived = pl.pallas_call(
        lambda *refs: scatter_kernel(n_sq, n_sw, *refs),
        out_shape=jax.ShapeDtypeStruct((n_dev, flat_rows, half), jnp.bfloat16),
        in_specs=[pl.BlockSpec(memory_space=pl.ANY)] * 3,
        out_specs=pl.BlockSpec(memory_space=pl.ANY),
        scratch_shapes=[
            pltpu.SemaphoreType.DMA((2 * (n_sq + n_sw),)),
            pltpu.SemaphoreType.DMA((1,)),
        ],
        input_output_aliases={2: 0},
        compiler_params=pltpu.CompilerParams(collective_id=0, has_side_effects=True),
    )(sq_pieces, sw_pieces, jnp.zeros((n_dev, flat_rows, half), jnp.bfloat16))

    is_sq = d < n_sq
    is_sw = (d >= n_sq) & (d < n_sq + n_sw)
    factor = jnp.where(is_sq, jnp.float32(math.sqrt(D)), jnp.float32(math.sqrt(FF)))
    iterate, first_scale = orthogonalize(arrived.reshape(D, half), factor)

    returned_sq, returned_sw = pl.pallas_call(
        lambda *refs: gather_kernel(n_sq, n_sw, *refs),
        out_shape=(
            jax.ShapeDtypeStruct((n_sq, out_rows, D // 2), jnp.bfloat16),
            jax.ShapeDtypeStruct((n_sw, out_rows, FF // 2), jnp.bfloat16),
        ),
        in_specs=[pl.BlockSpec(memory_space=pl.ANY)],
        out_specs=(pl.BlockSpec(memory_space=pl.ANY), pl.BlockSpec(memory_space=pl.ANY)),
        scratch_shapes=[
            pltpu.SemaphoreType.DMA((wide_count,)),
            pltpu.SemaphoreType.DMA((2,)),
        ],
        compiler_params=pltpu.CompilerParams(collective_id=1, has_side_effects=True),
    )(iterate.reshape(wide_count, out_rows, half))

    inv_sq = inverse_of(square_order)
    inv_sw = inverse_of(swiglu_order)
    square_update = returned_sq[inv_sq]
    swiglu_update = returned_sw[inv_sw]

    slots = jnp.arange(n_sq + n_sw, dtype=jnp.int32)
    mine = (t == 0) & (slots == d)
    slot_norms = lax.psum(jnp.where(mine, 0.5 * jnp.log(first_scale), 0.0), ("dp", "tensor"))
    matrix_slot = jnp.concatenate([inv_sq, n_sq + inv_sw])
    matrix_norms = slot_norms[matrix_slot]
    owner_norms = jnp.sum(jnp.where(owners == d, matrix_norms, 0.0)).reshape(1)

    vector_step, first_vector, second_vector = adamw_terms(
        vector_values, vector_grad, vector_first, vector_second
    )
    embed_rows = embed_values.shape[0]
    row_numbers = d * embed_rows + jnp.arange(embed_rows, dtype=jnp.int32)
    inside = (row_numbers[:, None] >= embed_ranges[None, :, 0]) & (
        row_numbers[:, None] < embed_ranges[None, :, 1]
    )
    row_live = jnp.sum(inside.astype(jnp.int32), axis=1) > 0
    direction, first_next, second_next = adamw_terms(
        embed_values, embed_grad, embed_first, embed_second
    )
    embed_step = jnp.where(row_live[:, None], direction, 0.0)
    first_embed = jnp.where(row_live[:, None], first_next, embed_first)
    second_embed = jnp.where(row_live[:, None], second_next, embed_second)
    return (
        square_next,
        swiglu_next,
        square_update,
        swiglu_update,
        owner_norms,
        vector_step,
        first_vector,
        second_vector,
        embed_step,
        first_embed,
        second_embed,
    )


def solution(mesh):
    placed = (
        P(None, ("dp", "tensor")),
        P(None, ("dp", "tensor")),
        P(None, ("dp", "tensor")),
        P(None, ("dp", "tensor")),
        P(),
        P(),
        P(),
        P(("dp", "tensor")),
        P(("dp", "tensor")),
        P(("dp", "tensor")),
        P(("dp", "tensor")),
        P("dp", "tensor"),
        P("dp", "tensor"),
        P("dp", "tensor"),
        P("dp", "tensor"),
        P(),
    )
    return jax.shard_map(
        local,
        mesh=mesh,
        in_specs=placed,
        out_specs=(
            P(None, ("dp", "tensor")),
            P(None, ("dp", "tensor")),
            P(None, "dp", "tensor"),
            P(None, "dp", "tensor"),
            P("dp"),
            P(("dp", "tensor")),
            P(("dp", "tensor")),
            P(("dp", "tensor")),
            P("dp", "tensor"),
            P("dp", "tensor"),
            P("dp", "tensor"),
        ),
        check_vma=False,
    )
```

time: 585 us -> 571 us (0.976)
  the two profiles are of different devices: /device:TPU:121 before, /device:TPU:64 now
where the time goes in v2:
time: 571 us; the launch traced here: 568 us
  Pallas kernels  238 us (42%)
  waiting for transfers between devices  109 us (19%)
  matrix products  79 us (14%)
  blocking collectives  68.5 us (12%)
  local copies, waits for them, and re-layouts  31.9 us (6%)
  other arithmetic  26.2 us (5%)
  between operations  15.2 us (3%)
    pallas_call x1, Pallas kernels, local(): pl.pallas_call(lambda *refs: scatter_kernel(n_sq, n_sw, *refs), out_shape...  136 us
    pallas_call x1, Pallas kernels, local(): pl.pallas_call(lambda *refs: gather_kernel(n_sq, n_sw, *refs), out_shape=...  101 us
    psum x1, blocking collectives, local(): lax.psum(jnp.where(mine, 0.5 * jnp.log(first_scale), 0.0), ('dp', 'tensor'))  65.4 us
    reduce_scatter x2, waiting for transfers between devices, orthogonalize(): lax.psum_scatter(jnp.einsum('rc,sc->rs', current, current, preferred_elem...  53.1 us
    all_gather x2, waiting for transfers between devices, orthogonalize(): lax.all_gather(normed_part, 'tensor', axis=0, tiled=True)  37.1 us
    dot_general x2, matrix products, orthogonalize(): jnp.dot(lax.all_gather(polynomial, 'tensor', axis=0, tiled=True), current...  31.7 us
    dot_general x2, matrix products, orthogonalize(): jnp.einsum('rc,sc->rs', current, current, preferred_element_type=jnp.floa...  29.2 us
    all_gather x2, waiting for transfers between devices, orthogonalize(): lax.all_gather(polynomial, 'tensor', axis=0, tiled=True)  18.4 us
  transfers between devices with their start and end apart: 6, of which 5 were waited for; matrix products, arithmetic and copies ran while one was open for 1% of the time, Pallas kernels for 0%

profile of v2, /device:TPU:64, one launch (start us, length us, event | category | flops | bytes accessed | tf_op | source)
XLA Modules:
  0.0 567.8 jit_solution(3350623533566724084)
XLA Ops:
  7.2 4.2 add_convert_fusion.3
  11.4 1.8 reshape.129.refs_0_
  13.1 6.7 %add_convert_fusion.2 = (bf16[24,49152]{1,0:T(8,128)(2,1)S(1)}, f32[24,49152]{1,0:T(8,128)}) fusion(f32[24,49152]{1,0:T(8,128)} %param.18, f32[24,49152]{1,0:T(8,128)} %param.19), kind=kLoop, calls=%fused_computation.11 | loop fusion | flops 5898240 | bytes 16515072 | tf_op jit(solution)/shard_map/convert_element_type | solution.py:25
  19.9 3.4 reshape.130.refs_1_
  23.2 4.3 broadcast_in_dim.52.clone.refs_2_
  27.5 136.4 %shard_map.239 = bf16[128,12,2048]{2,1,0:T(8,128)(2,1)} custom-call(bf16[32,12,1536]{2,1,0:T(8,128)(2,1)} %reshape.129.refs_0_, bf16[24,12,4096]{2,1,0:T(8,128)(2,1)} %reshape.130.refs_1_, bf16[128,12,2048]{2,1,0:T(8,128)(2,1)} %broadcast_in_dim.52.clone.refs_2_), custom_call_target="tpu_custom_call", output_to_operand_aliasing={{}: (2, {})} | custom-call | tf_op jit(solution)/shard_map/pallas_call | solution.py:320
  163.9 10.7 %reshape.131 = bf16[1536,2048]{1,0:T(8,128)(2,1)} reshape(bf16[128,12,2048]{2,1,0:T(8,128)(2,1)} %shard_map.239) | data formatting | bytes 12582912 | tf_op jit(solution)/shard_map/reshape | solution.py:336
  174.6 16.3 %fusion.11 = f32[1536,1536]{1,0:T(8,128)} fusion(bf16[1536,2048]{1,0:T(8,128)(2,1)} %reshape.131), kind=kOutput, calls=%fused_computation.47 | convolution fusion | flops 9663676416 | bytes 15728640 | tf_op jit(solution)/shard_map/rc,sc->rs/dot_general | solution.py:255
  191.0 31.1 %reduce-scatter.3.cloned.1.call-done = f32[768,1536]{1,0:T(8,128)} async-done(((f32[1536,1536]{1,0:T(8,128)}), f32[768,1536]{1,0:T(8,128)}) %reduce-scatter.3.cloned.1.call-update) | async-done | bytes 4718608 | tf_op jit(solution)/shard_map/reduce_scatter | solution.py:254
  222.1 4.2 multiply_reduce_fusion
  226.3 3.1 psum.14
  230.1 4.3 divide_convert_fusion.1
  234.4 18.6 %all-gather.5.cloned.1.call-done = bf16[1536,1536]{1,0:T(8,128)(2,1)} async-done(((bf16[768,1536]{1,0:T(8,128)(2,1)}), bf16[1536,1536]{1,0:T(8,128)(2,1)}) %all-gather.5.cloned.1.call-update) | async-done | bytes 4718608 | tf_op jit(solution)/shard_map/all_gather | solution.py:269
  253.0 9.1 %add_convert_fusion.1 = bf16[768,1536]{1,0:T(8,128)(2,1)} fusion(bf16[768,1536]{1,0:T(8,128)(2,1)} %divide_convert_fusion.1, bf16[1536,1536]{1,0:T(8,128)(2,1)} %all-gather.5.cloned.1.call-done), kind=kOutput, calls=%fused_computation.8 | convolution fusion | flops 3629776896 | bytes 9437184 | tf_op jit(solution)/shard_map/dot_general | solution.py:267
  262.4 18.4 %all-gather.7.cloned.1.call-done = bf16[1536,1536]{1,0:T(8,128)(2,1)} async-done(((bf16[768,1536]{1,0:T(8,128)(2,1)}), bf16[1536,1536]{1,0:T(8,128)(2,1)}) %all-gather.7.cloned.1.call-update) | async-done | bytes 4718608 | tf_op jit(solution)/shard_map/all_gather | solution.py:276
  280.7 15.0 %divide_convert_fusion = bf16[1536,2048]{1,0:T(8,128)(2,1)S(1)} fusion(bf16[1536,2048]{1,0:T(8,128)(2,1)} %reshape.131, bf16[1536,1536]{1,0:T(8,128)(2,1)} %all-gather.7.cloned.1.call-done, f32[]{:T(128)S(6)} %sqrt.13), kind=kOutput, calls=%fused_computation.6 | convolution fusion | flops 9679405056 | bytes 17301508 | tf_op jit(solution)/shard_map/dot_general | solution.py:275
  295.7 2.7 copy-done.12
  298.4 12.9 %fusion.12 = f32[1536,1536]{1,0:T(8,128)} fusion(bf16[1536,2048]{1,0:T(8,128)(2,1)S(1)} %divide_convert_fusion), kind=kOutput, calls=%fused_computation.48 | convolution fusion | flops 9663676416 | bytes 15728640 | tf_op jit(solution)/shard_map/rc,sc->rs/dot_general | solution.py:255
  311.4 22.0 %reduce-scatter.5.cloned.1.call-done = f32[768,1536]{1,0:T(8,128)} async-done(((f32[1536,1536]{1,0:T(8,128)}), f32[768,1536]{1,0:T(8,128)}) %reduce-scatter.5.cloned.1.call-update) | async-done | bytes 4718608 | tf_op jit(solution)/shard_map/reduce_scatter | solution.py:254
  333.3 4.0 convert_element_type.47
  337.6 18.5 %all-gather.9.cloned.1.call-done = bf16[1536,1536]{1,0:T(8,128)(2,1)} async-done(((bf16[768,1536]{1,0:T(8,128)(2,1)}), bf16[1536,1536]{1,0:T(8,128)(2,1)}) %all-gather.9.cloned.1.call-update) | async-done | bytes 4718608 | tf_op jit(solution)/shard_map/all_gather | solution.py:269
  356.1 9.1 %add_convert_fusion = bf16[768,1536]{1,0:T(8,128)(2,1)} fusion(bf16[768,1536]{1,0:T(8,128)(2,1)} %convert_element_type.47, bf16[1536,1536]{1,0:T(8,128)(2,1)} %all-gather.9.cloned.1.call-done), kind=kOutput, calls=%fused_computation.7 | convolution fusion | flops 3629776896 | bytes 9437184 | tf_op jit(solution)/shard_map/dot_general | solution.py:267
  365.2 0.7 scatter_custom_fusion
  366.0 0.9 scatter_custom_fusion.1
  367.1 0.6 multiply_add_fusion.3
  367.8 1.4 fusion.2
  369.3 65.4 %psum.15 = f32[56]{0:T(128)S(1)} all-reduce(f32[56]{0:T(128)S(1)} %and_select_fusion), channel_id=1, replica_groups=mesh['dp'=64,'tensor'=2] {'dp','tensor'}, use_global_device_ids=true, to_apply=%region_6.7 | all-reduce | flops 56 | bytes 448 | tf_op jit(solution)/shard_map/psum | solution.py:360
  434.7 0.8 gather_fusion.2
  436.1 16.7 %multiply_convert_fusion = bf16[1536,2048]{1,0:T(8,128)(2,1)} fusion(bf16[1536,2048]{1,0:T(8,128)(2,1)} %copy-done.12, bf16[1536,1536]{1,0:T(8,128)(2,1)} %all-gather.11.cloned.1.call-done, f32[]{:T(128)S(6)} %select_n.45), kind=kOutput, calls=%fused_computation.5 | convolution fusion | flops 9679405056 | bytes 17301508 | tf_op jit(solution)/shard_map/dot_general | solution.py:275
  452.8 101.4 %shard_map.240 = (bf16[32,24,768]{2,1,0:T(8,128)(2,1)}, bf16[24,24,2048]{2,1,0:T(8,128)(2,1)}) custom-call(bf16[64,24,2048]{2,1,0:T(8,128)(2,1)} %bitcast.23), custom_call_target="tpu_custom_call" | custom-call | tf_op jit(solution)/shard_map/pallas_call | solution.py:338
  554.2 2.9 gather_fusion
  557.1 3.8 gather_fusion.1
  (54 shorter events, 1.4 us)
Async XLA Ops:
  7.2 215.0 %reduce-scatter.3.cloned.1.call-start = ((), (), s32[]{:S(2)}) async-start(), calls=%async_computation.2 | async-start | bytes 14155776 | tf_op jit(solution)/shard_map/reduce_scatter | solution.py:254
  190.9 62.1 %all-gather.5.cloned.1.call-start = ((), (), s32[]{:S(2)}) async-start(), calls=%async_computation.3 | async-start | bytes 7077888 | tf_op jit(solution)/shard_map/all_gather | solution.py:269
  234.4 46.4 %all-gather.7.cloned.1.call-start = ((), (), s32[]{:S(2)}) async-start(), calls=%async_computation.4 | async-start | bytes 7077888 | tf_op jit(solution)/shard_map/all_gather | solution.py:276
  262.1 71.2 %reduce-scatter.5.cloned.1.call-start = ((), (), s32[]{:S(2)}) async-start(), calls=%async_computation.5 | async-start | bytes 14155776 | tf_op jit(solution)/shard_map/reduce_scatter | solution.py:254
  295.7 2.7 copy-start.12
  311.3 44.8 %all-gather.9.cloned.1.call-start = ((), (), s32[]{:S(2)}) async-start(), calls=%async_computation.6 | async-start | bytes 7077888 | tf_op jit(solution)/shard_map/all_gather | solution.py:269
  337.4 27.8 %copy-start.10 = (s32[32]{0:T(128)S(1)}, s32[32]{0:T(128)}, u32[]{:S(2)}) copy-start(s32[32]{0:T(128)} %param.20) | copy-start | bytes 388
  337.4 28.5 %copy-start.11 = (s32[24]{0:T(128)S(1)}, s32[24]{0:T(128)}, u32[]{:S(2)}) copy-start(s32[24]{0:T(128)} %param.21) | copy-start | bytes 292
  337.4 29.6 %copy-start.8 = (s32[16,2]{0,1:T(2,128)S(1)}, s32[16,2]{0,1:T(2,128)}, u32[]{:S(2)}) copy-start(s32[16,2]{0,1:T(2,128)} %param.31) | copy-start | bytes 388
  337.4 29.7 %copy-start.4 = (f32[1344]{0:T(1024)S(1)}, f32[1344]{0:T(1024)}, u32[]{:S(2)}) copy-start(f32[1344]{0:T(1024)} %param.23) | copy-start | bytes 16132
  337.4 29.7 %copy-start.5 = (f32[1344]{0:T(1024)S(1)}, f32[1344]{0:T(1024)}, u32[]{:S(2)}) copy-start(f32[1344]{0:T(1024)} %param.24) | copy-start | bytes 16132
  337.4 29.7 %copy-start.6 = (f32[1344]{0:T(1024)S(1)}, f32[1344]{0:T(1024)}, u32[]{:S(2)}) copy-start(f32[1344]{0:T(1024)} %param.25) | copy-start | bytes 16132
  337.5 29.7 %copy-start.7 = (f32[1344]{0:T(1024)S(1)}, f32[1344]{0:T(1024)}, u32[]{:S(2)}) copy-start(f32[1344]{0:T(1024)} %param.26) | copy-start | bytes 16132
  337.5 30.3 %copy-start = (f32[128,768]{1,0:T(8,128)S(1)}, f32[128,768]{1,0:T(8,128)}, u32[]{:S(2)}) copy-start(f32[128,768]{1,0:T(8,128)} %param.30) | copy-start | bytes 1179652
  337.5 30.3 %copy-start.1 = (f32[128,768]{1,0:T(8,128)S(1)}, f32[128,768]{1,0:T(8,128)}, u32[]{:S(2)}) copy-start(f32[128,768]{1,0:T(8,128)} %param.28) | copy-start | bytes 1179652
  337.5 30.3 %copy-start.2 = (f32[128,768]{1,0:T(8,128)S(1)}, f32[128,768]{1,0:T(8,128)}, u32[]{:S(2)}) copy-start(f32[128,768]{1,0:T(8,128)} %param.27) | copy-start | bytes 1179652
  337.5 30.3 %copy-start.3 = (f32[128,768]{1,0:T(8,128)S(1)}, f32[128,768]{1,0:T(8,128)}, u32[]{:S(2)}) copy-start(f32[128,768]{1,0:T(8,128)} %param.29) | copy-start | bytes 1179652
  337.5 98.6 %all-gather.11.cloned.1.call-start = ((), (), s32[]{:S(2)}) async-start(), calls=%async_computation.7 | async-start | bytes 7077888 | tf_op jit(solution)/shard_map/all_gather | solution.py:276
  365.2 70.3 %copy-start.9 = (s32[56]{0:T(128)S(1)}, s32[56]{0:T(128)}, u32[]{:S(2)}) copy-start(s32[56]{0:T(128)} %param.22) | copy-start | bytes 676
Sparse Core Ops, SparseCore 0:
  191.1 31.0 reduce-scatter.2
  234.5 18.4 all-gather.4
  262.2 18.4 all-gather.6
  311.4 21.8 reduce-scatter.4
  337.5 18.5 all-gather.8
  365.3 18.5 all-gather.10

commit v3 on v2

--- a/solution.py
+++ b/solution.py
@@ -283,6 +283,19 @@
         else:
             iterate = mixed.astype(jnp.bfloat16)
     return (iterate, first_scale)
+
+
+def with_scale_row(blocks, scale):
+    high = scale.astype(jnp.bfloat16)
+    low = (scale - high.astype(jnp.float32)).astype(jnp.bfloat16)
+    lanes = lax.broadcasted_iota(jnp.int32, (blocks.shape[0], 1, blocks.shape[2]), 2)
+    row = jnp.where(lanes == 0, high, jnp.where(lanes == 1, low, jnp.zeros((), jnp.bfloat16)))
+    return jnp.concatenate([blocks, row], axis=1)
+
+
+def scale_of_row(returned):
+    row = returned[:, -1, :2].astype(jnp.float32)
+    return row[:, 0] + row[:, 1]
 
 
 def local(
@@ -338,8 +351,8 @@
     returned_sq, returned_sw = pl.pallas_call(
         lambda *refs: gather_kernel(n_sq, n_sw, *refs),
         out_shape=(
-            jax.ShapeDtypeStruct((n_sq, out_rows, D // 2), jnp.bfloat16),
-            jax.ShapeDtypeStruct((n_sw, out_rows, FF // 2), jnp.bfloat16),
+            jax.ShapeDtypeStruct((n_sq, out_rows + 1, D // 2), jnp.bfloat16),
+            jax.ShapeDtypeStruct((n_sw, out_rows + 1, FF // 2), jnp.bfloat16),
         ),
         in_specs=[pl.BlockSpec(memory_space=pl.ANY)],
         out_specs=(pl.BlockSpec(memory_space=pl.ANY), pl.BlockSpec(memory_space=pl.ANY)),
@@ -348,16 +361,15 @@
             pltpu.SemaphoreType.DMA((2,)),
         ],
         compiler_params=pltpu.CompilerParams(collective_id=1, has_side_effects=True),
-    )(iterate.reshape(wide_count, out_rows, half))
+    )(with_scale_row(iterate.reshape(wide_count, out_rows, half), first_scale))
 
     inv_sq = inverse_of(square_order)
     inv_sw = inverse_of(swiglu_order)
-    square_update = returned_sq[inv_sq]
-    swiglu_update = returned_sw[inv_sw]
-
-    slots = jnp.arange(n_sq + n_sw, dtype=jnp.int32)
-    mine = (t == 0) & (slots == d)
-    slot_norms = lax.psum(jnp.where(mine, 0.5 * jnp.log(first_scale), 0.0), ("dp", "tensor"))
+    square_update = returned_sq[inv_sq][:, :out_rows]
+    swiglu_update = returned_sw[inv_sw][:, :out_rows]
+
+    slot_scales = jnp.concatenate([scale_of_row(returned_sq), scale_of_row(returned_sw)])
+    slot_norms = 0.5 * jnp.log(slot_scales)
     matrix_slot = jnp.concatenate([inv_sq, n_sq + inv_sw])
     matrix_norms = slot_norms[matrix_slot]
     owner_norms = jnp.sum(jnp.where(owners == d, matrix_norms, 0.0)).reshape(1)

time: 571 us -> 572 us (level)
  blocking collectives: 68.5 us -> 3.08 us
  Pallas kernels: 238 us -> 285 us
  waiting for transfers between devices: 109 us -> 123 us
  other arithmetic: 26.2 us -> 32.8 us
    psum x1 -> x0, blocking collectives: 65.4 us -> none  [local(): lax.psum(jnp.where(mine, 0.5 * jnp.log(first_scale), 0.0), ('dp', 'tensor'))]
    pallas_call x1, Pallas kernels: 101 us -> 149 us  [local(): pl.pallas_call(lambda *refs: gather_kernel(n_sq, n_sw, *refs), out_shape=...]
    all_gather x2, waiting for transfers between devices: 18.4 us -> 32.7 us  [orthogonalize(): lax.all_gather(polynomial, 'tensor', axis=0, tiled=True)]
  transfers between devices with their start and end apart: 6 -> 6, of which waited for: 5 -> 6; matrix products, arithmetic and copies ran while one was open for 1% -> 1% of each run, Pallas kernels for 0% -> 0%
where the time goes in v3:
time: 572 us; the launch traced here: 570 us
  Pallas kernels  285 us (50%)
  waiting for transfers between devices  123 us (22%)
  matrix products  77.2 us (13%)
  other arithmetic  32.8 us (6%)
  local copies, waits for them, and re-layouts  32.7 us (6%)
  between operations  15.2 us (3%)
    pallas_call x1, Pallas kernels, local(): pl.pallas_call(lambda *refs: gather_kernel(n_sq, n_sw, *refs), out_shape=...  149 us
    pallas_call x1, Pallas kernels, local(): pl.pallas_call(lambda *refs: scatter_kernel(n_sq, n_sw, *refs), out_shape...  136 us
    reduce_scatter x2, waiting for transfers between devices, orthogonalize(): lax.psum_scatter(jnp.einsum('rc,sc->rs', current, current, preferred_elem...  53.1 us
    all_gather x2, waiting for transfers between devices, orthogonalize(): lax.all_gather(normed_part, 'tensor', axis=0, tiled=True)  37 us
    all_gather x2, waiting for transfers between devices, orthogonalize(): lax.all_gather(polynomial, 'tensor', axis=0, tiled=True)  32.7 us
    dot_general x2, matrix products, orthogonalize(): jnp.dot(lax.all_gather(polynomial, 'tensor', axis=0, tiled=True), current...  29.8 us
    dot_general x2, matrix products, orthogonalize(): jnp.einsum('rc,sc->rs', current, current, preferred_element_type=jnp.floa...  29.2 us
    dot_general x2, matrix products, orthogonalize(): jnp.dot(normed_part, lax.all_gather(normed_part, 'tensor', axis=0, tiled=...  18.2 us
  transfers between devices with their start and end apart: 6, of which 6 were waited for; matrix products, arithmetic and copies ran while one was open for 1% of the time, Pallas kernels for 0%

profile of v3, /device:TPU:64, one launch (start us, length us, event | category | flops | bytes accessed | tf_op | source)
XLA Modules:
  0.0 569.6 jit_solution(17307828749094092177)
XLA Ops:
  7.2 6.7 %add_convert_fusion.2 = (bf16[24,49152]{1,0:T(8,128)(2,1)S(1)}, f32[24,49152]{1,0:T(8,128)}) fusion(f32[24,49152]{1,0:T(8,128)} %param.18, f32[24,49152]{1,0:T(8,128)} %param.19), kind=kLoop, calls=%fused_computation.12 | loop fusion | flops 5898240 | bytes 16515072 | tf_op jit(solution)/shard_map/convert_element_type | solution.py:25
  13.9 3.3 reshape.172.refs_1_
  17.3 4.2 add_convert_fusion.3
  21.4 1.8 reshape.171.refs_0_
  23.2 4.3 broadcast_in_dim.58.clone.refs_2_
  27.5 136.4 %shard_map.239 = bf16[128,12,2048]{2,1,0:T(8,128)(2,1)} custom-call(bf16[32,12,1536]{2,1,0:T(8,128)(2,1)} %reshape.171.refs_0_, bf16[24,12,4096]{2,1,0:T(8,128)(2,1)} %reshape.172.refs_1_, bf16[128,12,2048]{2,1,0:T(8,128)(2,1)} %broadcast_in_dim.58.clone.refs_2_), custom_call_target="tpu_custom_call", output_to_operand_aliasing={{}: (2, {})} | custom-call | tf_op jit(solution)/shard_map/pallas_call | solution.py:333
  163.9 10.7 %reshape.173 = bf16[1536,2048]{1,0:T(8,128)(2,1)} reshape(bf16[128,12,2048]{2,1,0:T(8,128)(2,1)} %shard_map.239) | data formatting | bytes 12582912 | tf_op jit(solution)/shard_map/reshape | solution.py:349
  174.6 16.3 %fusion.13 = f32[1536,1536]{1,0:T(8,128)} fusion(bf16[1536,2048]{1,0:T(8,128)(2,1)} %reshape.173), kind=kOutput, calls=%fused_computation.57 | convolution fusion | flops 9663676416 | bytes 15728640 | tf_op jit(solution)/shard_map/rc,sc->rs/dot_general | solution.py:255
  191.0 31.0 %reduce-scatter.3.cloned.1.call-done = f32[768,1536]{1,0:T(8,128)} async-done(((f32[1536,1536]{1,0:T(8,128)}), f32[768,1536]{1,0:T(8,128)}) %reduce-scatter.3.cloned.1.call-update) | async-done | bytes 4718608 | tf_op jit(solution)/shard_map/reduce_scatter | solution.py:254
  222.1 4.2 multiply_reduce_fusion
  226.2 3.1 psum.7
  230.0 4.3 divide_convert_fusion.1
  234.4 18.7 %all-gather.5.cloned.1.call-done = bf16[1536,1536]{1,0:T(8,128)(2,1)} async-done(((bf16[768,1536]{1,0:T(8,128)(2,1)}), bf16[1536,1536]{1,0:T(8,128)(2,1)}) %all-gather.5.cloned.1.call-update) | async-done | bytes 4718608 | tf_op jit(solution)/shard_map/all_gather | solution.py:269
  253.0 9.1 %add_convert_fusion.1 = bf16[768,1536]{1,0:T(8,128)(2,1)} fusion(bf16[768,1536]{1,0:T(8,128)(2,1)} %divide_convert_fusion.1, bf16[1536,1536]{1,0:T(8,128)(2,1)} %all-gather.5.cloned.1.call-done), kind=kOutput, calls=%fused_computation.9 | convolution fusion | flops 3629776896 | bytes 9437184 | tf_op jit(solution)/shard_map/dot_general | solution.py:267
  262.4 18.4 %all-gather.7.cloned.1.call-done = bf16[1536,1536]{1,0:T(8,128)(2,1)} async-done(((bf16[768,1536]{1,0:T(8,128)(2,1)}), bf16[1536,1536]{1,0:T(8,128)(2,1)}) %all-gather.7.cloned.1.call-update) | async-done | bytes 4718608 | tf_op jit(solution)/shard_map/all_gather | solution.py:276
  280.8 14.9 %divide_convert_fusion = bf16[1536,2048]{1,0:T(8,128)(2,1)S(1)} fusion(bf16[1536,2048]{1,0:T(8,128)(2,1)} %reshape.173, bf16[1536,1536]{1,0:T(8,128)(2,1)} %all-gather.7.cloned.1.call-done, f32[]{:T(128)S(6)} %sqrt.13), kind=kOutput, calls=%fused_computation.6 | convolution fusion | flops 9679405056 | bytes 17301508 | tf_op jit(solution)/shard_map/dot_general | solution.py:275
  295.7 2.7 copy-done.12
  298.4 12.9 %fusion.14 = f32[1536,1536]{1,0:T(8,128)} fusion(bf16[1536,2048]{1,0:T(8,128)(2,1)S(1)} %divide_convert_fusion), kind=kOutput, calls=%fused_computation.58 | convolution fusion | flops 9663676416 | bytes 15728640 | tf_op jit(solution)/shard_map/rc,sc->rs/dot_general | solution.py:255
  311.3 22.1 %reduce-scatter.5.cloned.1.call-done = f32[768,1536]{1,0:T(8,128)} async-done(((f32[1536,1536]{1,0:T(8,128)}), f32[768,1536]{1,0:T(8,128)}) %reduce-scatter.5.cloned.1.call-update) | async-done | bytes 4718608 | tf_op jit(solution)/shard_map/reduce_scatter | solution.py:254
  333.4 4.0 convert_element_type.68
  337.6 18.4 %all-gather.9.cloned.1.call-done = bf16[1536,1536]{1,0:T(8,128)(2,1)} async-done(((bf16[768,1536]{1,0:T(8,128)(2,1)}), bf16[1536,1536]{1,0:T(8,128)(2,1)}) %all-gather.9.cloned.1.call-update) | async-done | bytes 4718608 | tf_op jit(solution)/shard_map/all_gather | solution.py:269
  356.0 9.1 %add_convert_fusion = bf16[768,1536]{1,0:T(8,128)(2,1)} fusion(bf16[768,1536]{1,0:T(8,128)(2,1)} %convert_element_type.68, bf16[1536,1536]{1,0:T(8,128)(2,1)} %all-gather.9.cloned.1.call-done), kind=kOutput, calls=%fused_computation.8 | convolution fusion | flops 3629776896 | bytes 9437184 | tf_op jit(solution)/shard_map/dot_general | solution.py:267
  365.8 0.9 scatter_custom_fusion
  367.6 1.4 fusion.2
  369.3 14.3 %all-gather.11.cloned.1.call-done = bf16[1536,1536]{1,0:T(8,128)(2,1)} async-done(((bf16[768,1536]{1,0:T(8,128)(2,1)}), bf16[1536,1536]{1,0:T(8,128)(2,1)}) %all-gather.11.cloned.1.call-update) | async-done | bytes 4718608 | tf_op jit(solution)/shard_map/all_gather | solution.py:276
  383.7 14.9 %multiply_convert_fusion = bf16[1536,2048]{1,0:T(8,128)(2,1)S(1)} fusion(bf16[1536,2048]{1,0:T(8,128)(2,1)} %copy-done.12, bf16[1536,1536]{1,0:T(8,128)(2,1)} %all-gather.11.cloned.1.call-done, f32[]{:T(128)S(6)} %select_n.58), kind=kOutput, calls=%fused_computation.5 | convolution fusion | flops 9679405056 | bytes 17301508 | tf_op jit(solution)/shard_map/dot_general | solution.py:275
  398.6 4.5 pad_maximum_fusion.refs_0_
  403.2 148.9 %shard_map.240 = (bf16[32,25,768]{2,1,0:T(8,128)(2,1)}, bf16[24,25,2048]{2,1,0:T(8,128)(2,1)}) custom-call(bf16[64,25,2048]{2,1,0:T(8,128)(2,1)} %pad_maximum_fusion.refs_0_), custom_call_target="tpu_custom_call" | custom-call | tf_op jit(solution)/shard_map/pallas_call | solution.py:351
  553.9 2.6 gather_fusion.1
  556.6 1.6 slice.47
  558.2 2.1 gather_fusion
  560.2 1.1 slice.46
  (65 shorter events, 5.7 us)
Async XLA Ops:
  7.2 214.9 %reduce-scatter.3.cloned.1.call-start = ((), (), s32[]{:S(2)}) async-start(), calls=%async_computation.2 | async-start | bytes 14155776 | tf_op jit(solution)/shard_map/reduce_scatter | solution.py:254
  191.0 62.0 %all-gather.5.cloned.1.call-start = ((), (), s32[]{:S(2)}) async-start(), calls=%async_computation.3 | async-start | bytes 7077888 | tf_op jit(solution)/shard_map/all_gather | solution.py:269
  234.3 46.4 %all-gather.7.cloned.1.call-start = ((), (), s32[]{:S(2)}) async-start(), calls=%async_computation.4 | async-start | bytes 7077888 | tf_op jit(solution)/shard_map/all_gather | solution.py:276
  262.1 71.2 %reduce-scatter.5.cloned.1.call-start = ((), (), s32[]{:S(2)}) async-start(), calls=%async_computation.5 | async-start | bytes 14155776 | tf_op jit(solution)/shard_map/reduce_scatter | solution.py:254
  295.7 2.7 copy-start.12
  311.2 44.7 %all-gather.9.cloned.1.call-start = ((), (), s32[]{:S(2)}) async-start(), calls=%async_computation.6 | async-start | bytes 7077888 | tf_op jit(solution)/shard_map/all_gather | solution.py:269
  337.4 27.7 %copy-start.10 = (s32[24]{0:T(128)S(1)}, s32[24]{0:T(128)}, u32[]{:S(2)}) copy-start(s32[24]{0:T(128)} %param.21) | copy-start | bytes 292
  337.4 28.3 %copy-start.11 = (s32[32]{0:T(128)S(1)}, s32[32]{0:T(128)}, u32[]{:S(2)}) copy-start(s32[32]{0:T(128)} %param.20) | copy-start | bytes 388
  337.4 29.4 %copy-start.8 = (s32[16,2]{0,1:T(2,128)S(1)}, s32[16,2]{0,1:T(2,128)}, u32[]{:S(2)}) copy-start(s32[16,2]{0,1:T(2,128)} %param.31) | copy-start | bytes 388
  337.4 29.5 %copy-start.4 = (f32[1344]{0:T(1024)S(1)}, f32[1344]{0:T(1024)}, u32[]{:S(2)}) copy-start(f32[1344]{0:T(1024)} %param.23) | copy-start | bytes 16132
  337.4 29.5 %copy-start.5 = (f32[1344]{0:T(1024)S(1)}, f32[1344]{0:T(1024)}, u32[]{:S(2)}) copy-start(f32[1344]{0:T(1024)} %param.24) | copy-start | bytes 16132
  337.5 29.5 %copy-start.6 = (f32[1344]{0:T(1024)S(1)}, f32[1344]{0:T(1024)}, u32[]{:S(2)}) copy-start(f32[1344]{0:T(1024)} %param.25) | copy-start | bytes 16132
  337.5 29.5 %copy-start.7 = (f32[1344]{0:T(1024)S(1)}, f32[1344]{0:T(1024)}, u32[]{:S(2)}) copy-start(f32[1344]{0:T(1024)} %param.26) | copy-start | bytes 16132
  337.5 30.1 %copy-start = (f32[128,768]{1,0:T(8,128)S(1)}, f32[128,768]{1,0:T(8,128)}, u32[]{:S(2)}) copy-start(f32[128,768]{1,0:T(8,128)} %param.30) | copy-start | bytes 1179652
  337.5 30.1 %copy-start.1 = (f32[128,768]{1,0:T(8,128)S(1)}, f32[128,768]{1,0:T(8,128)}, u32[]{:S(2)}) copy-start(f32[128,768]{1,0:T(8,128)} %param.28) | copy-start | bytes 1179652
  337.5 30.1 %copy-start.2 = (f32[128,768]{1,0:T(8,128)S(1)}, f32[128,768]{1,0:T(8,128)}, u32[]{:S(2)}) copy-start(f32[128,768]{1,0:T(8,128)} %param.27) | copy-start | bytes 1179652
  337.5 30.1 %copy-start.3 = (f32[128,768]{1,0:T(8,128)S(1)}, f32[128,768]{1,0:T(8,128)}, u32[]{:S(2)}) copy-start(f32[128,768]{1,0:T(8,128)} %param.29) | copy-start | bytes 1179652
  337.5 46.2 %all-gather.11.cloned.1.call-start = ((), (), s32[]{:S(2)}) async-start(), calls=%async_computation.7 | async-start | bytes 7077888 | tf_op jit(solution)/shard_map/all_gather | solution.py:276
  556.6 5.6 copy-start.9
Sparse Core Ops, SparseCore 0:
  191.1 30.9 reduce-scatter.2
  234.4 18.5 all-gather.4
  262.3 18.4 all-gather.6
  311.4 21.9 reduce-scatter.4
  337.5 18.3 all-gather.8
  365.2 18.4 all-gather.10

commit v4 on v3

--- a/solution.py
+++ b/solution.py
@@ -56,98 +56,121 @@
     pl.semaphore_wait(barrier, n_dev - 1)
 
 
-def scatter_kernel(n_sq, n_sw, sq_ref, sw_ref, zero_ref, out_ref, send_sem, recv_sem):
+def scatter_kernel(n_sq, n_sw, sq_ref, sw_ref, zero_ref, out_ref, comb_sq, comb_sw, send_sem, recv_sem, pair_sem):
     del zero_ref
     d = lax.axis_index("dp")
     t = lax.axis_index("tensor")
     n_dev = lax.axis_size("dp") * 2
+    n_slots = n_sq + n_sw
     me = d * 2 + t
-    n_pairs = 2 * (n_sq + n_sw)
-    sq_w = sq_ref.shape[2] // 2
-    sw_w = sw_ref.shape[2] // 2
+    sq_w = comb_sq.shape[3]
+    sw_w = comb_sw.shape[3]
     device_barrier(n_dev, me, True)
 
-    def sq_copy(g, h):
+    other = 1 - t
+    swap_sq = pltpu.make_async_remote_copy(
+        src_ref=sq_ref.at[:, :, pl.ds(pl.multiple_of(other * sq_w, 128), sq_w)],
+        dst_ref=comb_sq.at[:, t],
+        send_sem=pair_sem.at[0],
+        recv_sem=pair_sem.at[1],
+        device_id=(d, other),
+        device_id_type=MESH,
+    )
+    swap_sw = pltpu.make_async_remote_copy(
+        src_ref=sw_ref.at[:, :, pl.ds(pl.multiple_of(other * sw_w, 128), sw_w)],
+        dst_ref=comb_sw.at[:, t],
+        send_sem=pair_sem.at[2],
+        recv_sem=pair_sem.at[3],
+        device_id=(d, other),
+        device_id_type=MESH,
+    )
+    keep_sq = pltpu.make_async_copy(
+        sq_ref.at[:, :, pl.ds(pl.multiple_of(t * sq_w, 128), sq_w)], comb_sq.at[:, t], pair_sem.at[4]
+    )
+    keep_sw = pltpu.make_async_copy(
+        sw_ref.at[:, :, pl.ds(pl.multiple_of(t * sw_w, 128), sw_w)], comb_sw.at[:, t], pair_sem.at[5]
+    )
+    swap_sq.start()
+    swap_sw.start()
+    keep_sq.start()
+    keep_sw.start()
+    keep_sq.wait()
+    keep_sw.wait()
+    pltpu.make_async_copy(comb_sq.at[:, other], comb_sq.at[:, other], pair_sem.at[1]).wait()
+    pltpu.make_async_copy(comb_sw.at[:, other], comb_sw.at[:, other], pair_sem.at[3]).wait()
+    swap_sq.wait_send()
+    swap_sw.wait_send()
+
+    def sq_copy(g):
         return pltpu.make_async_remote_copy(
-            src_ref=sq_ref.at[g, :, pl.ds(pl.multiple_of(h * sq_w, 128), sq_w)],
-            dst_ref=out_ref.at[me, :, pl.ds(0, sq_w)],
-            send_sem=send_sem.at[2 * g + h],
+            src_ref=comb_sq.at[g],
+            dst_ref=out_ref.at[d, :, :, pl.ds(0, sq_w)],
+            send_sem=send_sem.at[g],
             recv_sem=recv_sem.at[0],
-            device_id=(g, h),
+            device_id=(g, t),
             device_id_type=MESH,
         )
 
-    def sw_copy(g, h):
-        j = g - n_sq
+    def sw_copy(g):
         return pltpu.make_async_remote_copy(
-            src_ref=sw_ref.at[j, :, pl.ds(pl.multiple_of(h * sw_w, 128), sw_w)],
-            dst_ref=out_ref.at[me, :, pl.ds(0, sw_w)],
-            send_sem=send_sem.at[2 * g + h],
+            src_ref=comb_sw.at[g - n_sq],
+            dst_ref=out_ref.at[d, :, :, pl.ds(0, sw_w)],
+            send_sem=send_sem.at[g],
             recv_sem=recv_sem.at[0],
-            device_id=(g, h),
+            device_id=(g, t),
             device_id_type=MESH,
         )
 
     def start(k, carry):
-        q = lax.rem(k + me, n_pairs)
-        g = q // 2
-        h = lax.rem(q, 2)
-        local = (g == d) & (h == t)
+        g = lax.rem(k + d, n_slots)
+        local = g == d
 
         @pl.when(local & (g < n_sq))
         def _():
             pltpu.make_async_copy(
-                sq_ref.at[g, :, pl.ds(pl.multiple_of(h * sq_w, 128), sq_w)],
-                out_ref.at[me, :, pl.ds(0, sq_w)],
-                recv_sem.at[0],
+                comb_sq.at[g], out_ref.at[d, :, :, pl.ds(0, sq_w)], recv_sem.at[0]
             ).start()
 
         @pl.when(local & (g >= n_sq))
         def _():
             pltpu.make_async_copy(
-                sw_ref.at[g - n_sq, :, pl.ds(pl.multiple_of(h * sw_w, 128), sw_w)],
-                out_ref.at[me, :, pl.ds(0, sw_w)],
-                recv_sem.at[0],
+                comb_sw.at[g - n_sq], out_ref.at[d, :, :, pl.ds(0, sw_w)], recv_sem.at[0]
             ).start()
 
         @pl.when(jnp.logical_not(local) & (g < n_sq))
         def _():
-            sq_copy(g, h).start()
+            sq_copy(g).start()
 
         @pl.when(jnp.logical_not(local) & (g >= n_sq))
         def _():
-            sw_copy(g, h).start()
+            sw_copy(g).start()
 
         return carry
 
-    lax.fori_loop(0, n_pairs, start, 0)
+    lax.fori_loop(0, n_slots, start, 0)
 
     @pl.when(d < n_sq)
     def _():
-        region = out_ref.at[:, :, pl.ds(0, sq_w)]
+        region = out_ref.at[:, :, :, pl.ds(0, sq_w)]
         pltpu.make_async_copy(region, region, recv_sem.at[0]).wait()
 
-    @pl.when((d >= n_sq) & (d < n_sq + n_sw))
-    def _():
-        region = out_ref.at[:, :, pl.ds(0, sw_w)]
+    @pl.when((d >= n_sq) & (d < n_slots))
+    def _():
+        region = out_ref.at[:, :, :, pl.ds(0, sw_w)]
         pltpu.make_async_copy(region, region, recv_sem.at[0]).wait()
 
-    def wait(q, carry):
-        g = q // 2
-        h = lax.rem(q, 2)
-        local = (g == d) & (h == t)
-
-        @pl.when(jnp.logical_not(local) & (g < n_sq))
-        def _():
-            sq_copy(g, h).wait_send()
-
-        @pl.when(jnp.logical_not(local) & (g >= n_sq))
-        def _():
-            sw_copy(g, h).wait_send()
+    def wait(g, carry):
+        @pl.when((g != d) & (g < n_sq))
+        def _():
+            sq_copy(g).wait_send()
+
+        @pl.when((g != d) & (g >= n_sq))
+        def _():
+            sw_copy(g).wait_send()
 
         return carry
 
-    lax.fori_loop(0, n_pairs, wait, 0)
+    lax.fori_loop(0, n_slots, wait, 0)
 
 
 def gather_kernel(n_sq, n_sw, it_ref, osq_ref, osw_ref, send_sem, recv_sem):
@@ -332,16 +355,19 @@
     half = FF // 2
     arrived = pl.pallas_call(
         lambda *refs: scatter_kernel(n_sq, n_sw, *refs),
-        out_shape=jax.ShapeDtypeStruct((n_dev, flat_rows, half), jnp.bfloat16),
+        out_shape=jax.ShapeDtypeStruct((wide_count, 2, flat_rows, half), jnp.bfloat16),
         in_specs=[pl.BlockSpec(memory_space=pl.ANY)] * 3,
         out_specs=pl.BlockSpec(memory_space=pl.ANY),
         scratch_shapes=[
-            pltpu.SemaphoreType.DMA((2 * (n_sq + n_sw),)),
+            pltpu.VMEM((n_sq, 2, flat_rows, D // 2), jnp.bfloat16),
+            pltpu.VMEM((n_sw, 2, flat_rows, half), jnp.bfloat16),
+            pltpu.SemaphoreType.DMA((n_sq + n_sw,)),
             pltpu.SemaphoreType.DMA((1,)),
+            pltpu.SemaphoreType.DMA((6,)),
         ],
         input_output_aliases={2: 0},
         compiler_params=pltpu.CompilerParams(collective_id=0, has_side_effects=True),
-    )(sq_pieces, sw_pieces, jnp.zeros((n_dev, flat_rows, half), jnp.bfloat16))
+    )(sq_pieces, sw_pieces, jnp.zeros((wide_count, 2, flat_rows, half), jnp.bfloat16))
 
     is_sq = d < n_sq
     is_sw = (d >= n_sq) & (d < n_sq + n_sw)

time: 572 us -> 574 us (level)
  waiting for transfers between devices: 123 us -> 156 us
  Pallas kernels: 285 us -> 254 us
    reduce_scatter x2, waiting for transfers between devices: 53.1 us -> 86.3 us  [orthogonalize(): lax.psum_scatter(jnp.einsum('rc,sc->rs', current, current, preferred_elem...]
    pallas_call x1, Pallas kernels: 136 us -> 105 us  [local(): pl.pallas_call(lambda *refs: scatter_kernel(n_sq, n_sw, *refs), out_shape...]
where the time goes in v4:
time: 574 us; the launch traced here: 572 us
  Pallas kernels  254 us (44%)
  waiting for transfers between devices  156 us (27%)
  matrix products  77.2 us (13%)
  other arithmetic  32.8 us (6%)
  local copies, waits for them, and re-layouts  32.7 us (6%)
  between operations  15.2 us (3%)
    pallas_call x1, Pallas kernels, local(): pl.pallas_call(lambda *refs: gather_kernel(n_sq, n_sw, *refs), out_shape=...  149 us
    pallas_call x1, Pallas kernels, local(): pl.pallas_call(lambda *refs: scatter_kernel(n_sq, n_sw, *refs), out_shape...  105 us
    reduce_scatter x2, waiting for transfers between devices, orthogonalize(): lax.psum_scatter(jnp.einsum('rc,sc->rs', current, current, preferred_elem...  86.3 us
    all_gather x2, waiting for transfers between devices, orthogonalize(): lax.all_gather(normed_part, 'tensor', axis=0, tiled=True)  36.9 us
    all_gather x2, waiting for transfers between devices, orthogonalize(): lax.all_gather(polynomial, 'tensor', axis=0, tiled=True)  32.7 us
    dot_general x2, matrix products, orthogonalize(): jnp.dot(lax.all_gather(polynomial, 'tensor', axis=0, tiled=True), current...  29.8 us
    dot_general x2, matrix products, orthogonalize(): jnp.einsum('rc,sc->rs', current, current, preferred_element_type=jnp.floa...  29.2 us
    dot_general x2, matrix products, orthogonalize(): jnp.dot(normed_part, lax.all_gather(normed_part, 'tensor', axis=0, tiled=...  18.2 us
  transfers between devices with their start and end apart: 6, of which 6 were waited for; matrix products, arithmetic and copies ran while one was open for 1% of the time, Pallas kernels for 0%

profile of v4, /device:TPU:64, one launch (start us, length us, event | category | flops | bytes accessed | tf_op | source)
XLA Modules:
  0.0 571.8 jit_solution(5121251697895068051)
XLA Ops:
  7.2 6.7 %add_convert_fusion.2 = (bf16[24,49152]{1,0:T(8,128)(2,1)S(1)}, f32[24,49152]{1,0:T(8,128)}) fusion(f32[24,49152]{1,0:T(8,128)} %param.18, f32[24,49152]{1,0:T(8,128)} %param.19), kind=kLoop, calls=%fused_computation.12 | loop fusion | flops 5898240 | bytes 16515072 | tf_op jit(solution)/shard_map/convert_element_type | solution.py:25
  13.9 3.3 reshape.172.refs_1_
  17.3 4.2 add_convert_fusion.3
  21.4 1.8 reshape.171.refs_0_
  23.2 4.3 broadcast_in_dim.58.clone.refs_2_
  27.5 105.4 %shard_map.239 = bf16[64,2,12,2048]{3,2,1,0:T(8,128)(2,1)} custom-call(bf16[32,12,1536]{2,1,0:T(8,128)(2,1)} %reshape.171.refs_0_, bf16[24,12,4096]{2,1,0:T(8,128)(2,1)} %reshape.172.refs_1_, bf16[64,2,12,2048]{3,2,1,0:T(8,128)(2,1)} %broadcast_in_dim.58.clone.refs_2_), custom_call_target="tpu_custom_call", output_to_operand_aliasing={{}: (2, {})} | custom-call | tf_op jit(solution)/shard_map/pallas_call | solution.py:356
  132.9 10.7 %reshape.173 = bf16[1536,2048]{1,0:T(8,128)(2,1)} reshape(bf16[64,2,12,2048]{3,2,1,0:T(8,128)(2,1)} %shard_map.239) | data formatting | bytes 12582912 | tf_op jit(solution)/shard_map/reshape | solution.py:375
  143.6 16.3 %fusion.13 = f32[1536,1536]{1,0:T(8,128)} fusion(bf16[1536,2048]{1,0:T(8,128)(2,1)} %reshape.173), kind=kOutput, calls=%fused_computation.57 | convolution fusion | flops 9663676416 | bytes 15728640 | tf_op jit(solution)/shard_map/rc,sc->rs/dot_general | solution.py:278
  160.0 64.3 %reduce-scatter.3.cloned.1.call-done = f32[768,1536]{1,0:T(8,128)} async-done(((f32[1536,1536]{1,0:T(8,128)}), f32[768,1536]{1,0:T(8,128)}) %reduce-scatter.3.cloned.1.call-update) | async-done | bytes 4718608 | tf_op jit(solution)/shard_map/reduce_scatter | solution.py:277
  224.3 4.2 multiply_reduce_fusion
  228.5 3.1 psum.7
  232.2 4.3 divide_convert_fusion.1
  236.6 18.6 %all-gather.5.cloned.1.call-done = bf16[1536,1536]{1,0:T(8,128)(2,1)} async-done(((bf16[768,1536]{1,0:T(8,128)(2,1)}), bf16[1536,1536]{1,0:T(8,128)(2,1)}) %all-gather.5.cloned.1.call-update) | async-done | bytes 4718608 | tf_op jit(solution)/shard_map/all_gather | solution.py:292
  255.2 9.1 %add_convert_fusion.1 = bf16[768,1536]{1,0:T(8,128)(2,1)} fusion(bf16[768,1536]{1,0:T(8,128)(2,1)} %divide_convert_fusion.1, bf16[1536,1536]{1,0:T(8,128)(2,1)} %all-gather.5.cloned.1.call-done), kind=kOutput, calls=%fused_computation.9 | convolution fusion | flops 3629776896 | bytes 9437184 | tf_op jit(solution)/shard_map/dot_general | solution.py:290
  264.6 18.3 %all-gather.7.cloned.1.call-done = bf16[1536,1536]{1,0:T(8,128)(2,1)} async-done(((bf16[768,1536]{1,0:T(8,128)(2,1)}), bf16[1536,1536]{1,0:T(8,128)(2,1)}) %all-gather.7.cloned.1.call-update) | async-done | bytes 4718608 | tf_op jit(solution)/shard_map/all_gather | solution.py:299
  282.9 14.9 %divide_convert_fusion = bf16[1536,2048]{1,0:T(8,128)(2,1)S(1)} fusion(bf16[1536,2048]{1,0:T(8,128)(2,1)} %reshape.173, bf16[1536,1536]{1,0:T(8,128)(2,1)} %all-gather.7.cloned.1.call-done, f32[]{:T(128)S(6)} %sqrt.13), kind=kOutput, calls=%fused_computation.6 | convolution fusion | flops 9679405056 | bytes 17301508 | tf_op jit(solution)/shard_map/dot_general | solution.py:298
  297.8 2.7 copy-done.12
  300.5 12.9 %fusion.14 = f32[1536,1536]{1,0:T(8,128)} fusion(bf16[1536,2048]{1,0:T(8,128)(2,1)S(1)} %divide_convert_fusion), kind=kOutput, calls=%fused_computation.58 | convolution fusion | flops 9663676416 | bytes 15728640 | tf_op jit(solution)/shard_map/rc,sc->rs/dot_general | solution.py:278
  313.4 22.1 %reduce-scatter.5.cloned.1.call-done = f32[768,1536]{1,0:T(8,128)} async-done(((f32[1536,1536]{1,0:T(8,128)}), f32[768,1536]{1,0:T(8,128)}) %reduce-scatter.5.cloned.1.call-update) | async-done | bytes 4718608 | tf_op jit(solution)/shard_map/reduce_scatter | solution.py:277
  335.5 4.0 convert_element_type.68
  339.7 18.4 %all-gather.9.cloned.1.call-done = bf16[1536,1536]{1,0:T(8,128)(2,1)} async-done(((bf16[768,1536]{1,0:T(8,128)(2,1)}), bf16[1536,1536]{1,0:T(8,128)(2,1)}) %all-gather.9.cloned.1.call-update) | async-done | bytes 4718608 | tf_op jit(solution)/shard_map/all_gather | solution.py:292
  358.1 9.1 %add_convert_fusion = bf16[768,1536]{1,0:T(8,128)(2,1)} fusion(bf16[768,1536]{1,0:T(8,128)(2,1)} %convert_element_type.68, bf16[1536,1536]{1,0:T(8,128)(2,1)} %all-gather.9.cloned.1.call-done), kind=kOutput, calls=%fused_computation.8 | convolution fusion | flops 3629776896 | bytes 9437184 | tf_op jit(solution)/shard_map/dot_general | solution.py:290
  367.9 0.9 scatter_custom_fusion
  369.8 1.4 fusion.2
  371.5 14.3 %all-gather.11.cloned.1.call-done = bf16[1536,1536]{1,0:T(8,128)(2,1)} async-done(((bf16[768,1536]{1,0:T(8,128)(2,1)}), bf16[1536,1536]{1,0:T(8,128)(2,1)}) %all-gather.11.cloned.1.call-update) | async-done | bytes 4718608 | tf_op jit(solution)/shard_map/all_gather | solution.py:299
  385.8 14.9 %multiply_convert_fusion = bf16[1536,2048]{1,0:T(8,128)(2,1)S(1)} fusion(bf16[1536,2048]{1,0:T(8,128)(2,1)} %copy-done.12, bf16[1536,1536]{1,0:T(8,128)(2,1)} %all-gather.11.cloned.1.call-done, f32[]{:T(128)S(6)} %select_n.58), kind=kOutput, calls=%fused_computation.5 | convolution fusion | flops 9679405056 | bytes 17301508 | tf_op jit(solution)/shard_map/dot_general | solution.py:298
  400.8 4.5 pad_maximum_fusion.refs_0_
  405.3 148.9 %shard_map.240 = (bf16[32,25,768]{2,1,0:T(8,128)(2,1)}, bf16[24,25,2048]{2,1,0:T(8,128)(2,1)}) custom-call(bf16[64,25,2048]{2,1,0:T(8,128)(2,1)} %pad_maximum_fusion.refs_0_), custom_call_target="tpu_custom_call" | custom-call | tf_op jit(solution)/shard_map/pallas_call | solution.py:377
  556.1 2.6 gather_fusion.1
  558.7 1.6 slice.47
  560.3 2.1 gather_fusion
  562.3 1.1 slice.46
  (65 shorter events, 5.7 us)
Async XLA Ops:
  7.2 217.1 %reduce-scatter.3.cloned.1.call-start = ((), (), s32[]{:S(2)}) async-start(), calls=%async_computation.2 | async-start | bytes 14155776 | tf_op jit(solution)/shard_map/reduce_scatter | solution.py:277
  160.0 95.2 %all-gather.5.cloned.1.call-start = ((), (), s32[]{:S(2)}) async-start(), calls=%async_computation.3 | async-start | bytes 7077888 | tf_op jit(solution)/shard_map/all_gather | solution.py:292
  236.5 46.4 %all-gather.7.cloned.1.call-start = ((), (), s32[]{:S(2)}) async-start(), calls=%async_computation.4 | async-start | bytes 7077888 | tf_op jit(solution)/shard_map/all_gather | solution.py:299
  264.3 71.2 %reduce-scatter.5.cloned.1.call-start = ((), (), s32[]{:S(2)}) async-start(), calls=%async_computation.5 | async-start | bytes 14155776 | tf_op jit(solution)/shard_map/reduce_scatter | solution.py:277
  297.8 2.7 copy-start.12
  313.4 44.7 %all-gather.9.cloned.1.call-start = ((), (), s32[]{:S(2)}) async-start(), calls=%async_computation.6 | async-start | bytes 7077888 | tf_op jit(solution)/shard_map/all_gather | solution.py:292
  339.5 27.7 %copy-start.10 = (s32[24]{0:T(128)S(1)}, s32[24]{0:T(128)}, u32[]{:S(2)}) copy-start(s32[24]{0:T(128)} %param.21) | copy-start | bytes 292
  339.5 28.3 %copy-start.11 = (s32[32]{0:T(128)S(1)}, s32[32]{0:T(128)}, u32[]{:S(2)}) copy-start(s32[32]{0:T(128)} %param.20) | copy-start | bytes 388
  339.6 29.4 %copy-start.8 = (s32[16,2]{0,1:T(2,128)S(1)}, s32[16,2]{0,1:T(2,128)}, u32[]{:S(2)}) copy-start(s32[16,2]{0,1:T(2,128)} %param.31) | copy-start | bytes 388
  339.6 29.5 %copy-start.4 = (f32[1344]{0:T(1024)S(1)}, f32[1344]{0:T(1024)}, u32[]{:S(2)}) copy-start(f32[1344]{0:T(1024)} %param.23) | copy-start | bytes 16132
  339.6 29.5 %copy-start.5 = (f32[1344]{0:T(1024)S(1)}, f32[1344]{0:T(1024)}, u32[]{:S(2)}) copy-start(f32[1344]{0:T(1024)} %param.24) | copy-start | bytes 16132
  339.6 29.5 %copy-start.6 = (f32[1344]{0:T(1024)S(1)}, f32[1344]{0:T(1024)}, u32[]{:S(2)}) copy-start(f32[1344]{0:T(1024)} %param.25) | copy-start | bytes 16132
  339.6 29.5 %copy-start.7 = (f32[1344]{0:T(1024)S(1)}, f32[1344]{0:T(1024)}, u32[]{:S(2)}) copy-start(f32[1344]{0:T(1024)} %param.26) | copy-start | bytes 16132
  339.6 30.1 %copy-start = (f32[128,768]{1,0:T(8,128)S(1)}, f32[128,768]{1,0:T(8,128)}, u32[]{:S(2)}) copy-start(f32[128,768]{1,0:T(8,128)} %param.30) | copy-start | bytes 1179652
  339.6 30.1 %copy-start.1 = (f32[128,768]{1,0:T(8,128)S(1)}, f32[128,768]{1,0:T(8,128)}, u32[]{:S(2)}) copy-start(f32[128,768]{1,0:T(8,128)} %param.28) | copy-start | bytes 1179652
  339.6 30.1 %copy-start.2 = (f32[128,768]{1,0:T(8,128)S(1)}, f32[128,768]{1,0:T(8,128)}, u32[]{:S(2)}) copy-start(f32[128,768]{1,0:T(8,128)} %param.27) | copy-start | bytes 1179652
  339.7 30.1 %copy-start.3 = (f32[128,768]{1,0:T(8,128)S(1)}, f32[128,768]{1,0:T(8,128)}, u32[]{:S(2)}) copy-start(f32[128,768]{1,0:T(8,128)} %param.29) | copy-start | bytes 1179652
  339.7 46.2 %all-gather.11.cloned.1.call-start = ((), (), s32[]{:S(2)}) async-start(), calls=%async_computation.7 | async-start | bytes 7077888 | tf_op jit(solution)/shard_map/all_gather | solution.py:299
  558.7 5.6 copy-start.9
Sparse Core Ops, SparseCore 0:
  160.1 64.1 reduce-scatter.2
  236.7 18.4 all-gather.4
  264.4 18.4 all-gather.6
  313.5 21.9 reduce-scatter.4
  339.7 18.3 all-gather.8
  367.3 18.4 all-gather.10

commit v5 on v4

--- a/solution.py
+++ b/solution.py
@@ -269,17 +269,28 @@
         lax.fori_loop(0, n_dp, wait, 0)
 
 
+def swap_halves(x):
+    return lax.ppermute(x, "tensor", perm=[(0, 1), (1, 0)])
+
+
 def orthogonalize(arrived, factor):
+    t = lax.axis_index("tensor")
+    rows = arrived.shape[0] // 2
+    mine = pl.multiple_of(t * rows, rows)
+    theirs = pl.multiple_of((1 - t) * rows, rows)
     iterate = arrived
     first_scale = jnp.float32(1.0)
     for round_index in range(NS_STEPS):
         current = iterate
-        gram_part = lax.psum_scatter(
-            jnp.einsum("rc,sc->rs", current, current, preferred_element_type=jnp.float32),
-            "tensor",
-            scatter_dimension=0,
-            tiled=True,
-        )
+        their_rows = lax.dynamic_slice_in_dim(current, theirs, rows, 0)
+        my_rows = lax.dynamic_slice_in_dim(current, mine, rows, 0)
+        sent = swap_halves(
+            jnp.einsum("rc,sc->rs", their_rows, current, preferred_element_type=jnp.float32)
+        )
+        kept = lax.optimization_barrier(
+            jnp.einsum("rc,sc->rs", my_rows, current, preferred_element_type=jnp.float32)
+        )
+        gram_part = kept + sent
         if round_index == 0:
             squares_total = lax.psum(jnp.sum(gram_part * gram_part), "tensor")
             gram_scale = jnp.sqrt(squares_total) + 1e-06
@@ -287,18 +298,33 @@
         else:
             gram_scale = jnp.float32(1.0)
         normed_part = (gram_part / gram_scale).astype(jnp.bfloat16)
-        squared = jnp.dot(
-            normed_part,
-            lax.all_gather(normed_part, "tensor", axis=0, tiled=True),
+        normed_other = swap_halves(normed_part)
+        squared = lax.optimization_barrier(
+            jnp.dot(
+                lax.dynamic_slice_in_dim(normed_part, mine, rows, 1),
+                normed_part,
+                preferred_element_type=jnp.float32,
+            )
+        ) + jnp.dot(
+            lax.dynamic_slice_in_dim(normed_part, theirs, rows, 1),
+            normed_other,
             preferred_element_type=jnp.float32,
         )
         polynomial = (
             QUINTIC_CUBIC * normed_part.astype(jnp.float32) + QUINTIC_FIFTH * squared
         ).astype(jnp.bfloat16)
-        product = jnp.dot(
-            lax.all_gather(polynomial, "tensor", axis=0, tiled=True),
-            current,
-            preferred_element_type=jnp.float32,
+        poly_other = swap_halves(polynomial)
+        product_mine = lax.optimization_barrier(
+            jnp.dot(polynomial, current, preferred_element_type=jnp.float32)
+        )
+        product_other = jnp.dot(poly_other, current, preferred_element_type=jnp.float32)
+        first = t == 0
+        product = jnp.concatenate(
+            [
+                jnp.where(first, product_mine, product_other),
+                jnp.where(first, product_other, product_mine),
+            ],
+            axis=0,
         )
         mixed = (QUINTIC_LINEAR * current.astype(jnp.float32) + product) / jnp.sqrt(gram_scale)
         if round_index == NS_STEPS - 1:

time: 574 us -> 532 us (0.927)
  waiting for transfers between devices: 156 us -> 2.38 us
  other arithmetic: 32.8 us -> 96.8 us
  Pallas kernels: 254 us -> 297 us
  local copies, waits for them, and re-layouts: 32.7 us -> 47.5 us
  between operations: 15.2 us -> 2.04 us
    reduce_scatter x2 -> x0, waiting for transfers between devices: 86.3 us -> none  [orthogonalize(): lax.psum_scatter(jnp.einsum('rc,sc->rs', current, current, preferred_elem...]
    all_gather x4 -> x0, waiting for transfers between devices: 69.6 us -> none  [the longest x2 36.9 us: orthogonalize(): lax.all_gather(normed_part, 'tensor', axis=0, tiled=True)]
    pallas_call x1, Pallas kernels: 149 us -> 191 us  [local(): pl.pallas_call(lambda *refs: gather_kernel(n_sq, n_sw, *refs), out_shape=...]
    convert_element_type x0 -> x3, other arithmetic: none -> 22.3 us  [the longest x1 16.1 us: orthogonalize(): iterate = (factor * mixed).astype(jnp.bfloat16)]
    concatenate x0 -> x2, other arithmetic: none -> 18 us  [orthogonalize(): jnp.concatenate([jnp.where(first, product_mine, product_other), jnp.where...]
    mul x0 -> x1, local copies, waits for them, and re-layouts: none -> 17.6 us  [orthogonalize(): QUINTIC_LINEAR * current.astype(jnp.float32) + product]
    select_n x0 -> x1, other arithmetic: none -> 11.9 us  [orthogonalize(): jnp.where(first, product_mine, product_other)]
    mul x0 -> x1, other arithmetic: none -> 11.7 us  [orthogonalize(): QUINTIC_LINEAR * current.astype(jnp.float32) + product]
  transfers between devices with their start and end apart: 6 -> 6, of which waited for: 6 -> 1; matrix products, arithmetic and copies ran while one was open for 1% -> 13% of each run, Pallas kernels for 0% -> 0%
where the time goes in v5:
time: 532 us; the launch traced here: 524 us
  Pallas kernels  297 us (56%)
  other arithmetic  96.8 us (18%)
  matrix products  72.9 us (14%)
  local copies, waits for them, and re-layouts  47.5 us (9%)
    pallas_call x1, Pallas kernels, local(): pl.pallas_call(lambda *refs: gather_kernel(n_sq, n_sw, *refs), out_shape=...  191 us
    pallas_call x1, Pallas kernels, local(): pl.pallas_call(lambda *refs: scatter_kernel(n_sq, n_sw, *refs), out_shape...  105 us
    concatenate x2, other arithmetic, orthogonalize(): jnp.concatenate([jnp.where(first, product_mine, product_other), jnp.where...  18 us
    dot_general x2, matrix products, orthogonalize(): jnp.dot(polynomial, current, preferred_element_type=jnp.float32)  17.7 us
    mul x1, local copies, waits for them, and re-layouts, orthogonalize(): QUINTIC_LINEAR * current.astype(jnp.float32) + product  17.6 us
    dot_general x2, matrix products, orthogonalize(): jnp.einsum('rc,sc->rs', their_rows, current, preferred_element_type=jnp.f...  16.4 us
    convert_element_type x1, other arithmetic, orthogonalize(): iterate = (factor * mixed).astype(jnp.bfloat16)  16.1 us
    dot_general x2, matrix products, orthogonalize(): jnp.dot(poly_other, current, preferred_element_type=jnp.float32)  15.3 us
  transfers between devices with their start and end apart: 6, of which 1 were waited for; matrix products, arithmetic and copies ran while one was open for 13% of the time, Pallas kernels for 0%

profile of v5, /device:TPU:64, one launch (start us, length us, event | category | flops | bytes accessed | tf_op | source)
XLA Modules:
  0.0 524.4 jit_solution(10587255158800745867)
XLA Ops:
  0.7 6.7 %add_convert_fusion.3 = (bf16[24,49152]{1,0:T(8,128)(2,1)S(1)}, f32[24,49152]{1,0:T(8,128)}) fusion(f32[24,49152]{1,0:T(8,128)} %param.18, f32[24,49152]{1,0:T(8,128)} %param.19), kind=kLoop, calls=%fused_computation.19 | loop fusion | flops 5898240 | bytes 16515072 | tf_op jit(solution)/shard_map/convert_element_type | solution.py:25
  7.4 3.3 reshape.176.refs_1_
  10.7 4.2 add_convert_fusion.4
  16.6 4.4 broadcast_in_dim.58.clone.refs_2_
  21.0 105.4 %shard_map.239 = bf16[64,2,12,2048]{3,2,1,0:T(8,128)(2,1)} custom-call(bf16[32,12,1536]{2,1,0:T(8,128)(2,1)} %reshape.175.refs_0_, bf16[24,12,4096]{2,1,0:T(8,128)(2,1)} %reshape.176.refs_1_, bf16[64,2,12,2048]{3,2,1,0:T(8,128)(2,1)} %broadcast_in_dim.58.clone.refs_2_), custom_call_target="tpu_custom_call", output_to_operand_aliasing={{}: (2, {})} | custom-call | tf_op jit(solution)/shard_map/pallas_call | solution.py:382
  126.4 10.7 %reshape.177 = bf16[1536,2048]{1,0:T(8,128)(2,1)} reshape(bf16[64,2,12,2048]{3,2,1,0:T(8,128)(2,1)} %shard_map.239) | data formatting | bytes 12582912 | tf_op jit(solution)/shard_map/reshape | solution.py:401
  137.1 9.6 %fusion.6 = f32[768,1536]{1,0:T(8,128)} fusion(bf16[1536,2048]{1,0:T(8,128)(2,1)} %reshape.177, s32[]{:T(128)S(6)} %select_n.93), kind=kOutput, calls=%fused_computation.25 | convolution fusion | flops 4831838208 | bytes 14155780 | tf_op jit(solution)/shard_map/rc,sc->rs/dot_general | solution.py:288
  147.2 8.9 %fusion.8 = f32[768,1536]{1,0:T(8,128)S(1)} fusion(bf16[1536,2048]{1,0:T(8,128)(2,1)} %reshape.177, s32[]{:T(128)S(6)} %select_n.92), kind=kOutput, calls=%fused_computation.27 | convolution fusion | flops 4831838208 | bytes 14155780 | tf_op jit(solution)/shard_map/rc,sc->rs/dot_general | solution.py:291
  156.1 6.4 %multiply_reduce_fusion = (f32[]{:T(128)}, f32[768,1536]{1,0:T(8,128)}) fusion(f32[768,1536]{1,0:T(8,128)S(1)} %fusion.8, f32[768,1536]{1,0:T(8,128)} %collective-permute-done), kind=kLoop, calls=%fused_computation.18 | loop fusion | flops 3538943 | bytes 14155780 | tf_op jit(solution)/shard_map/reduce_sum | solution.py:295
  162.4 3.1 psum.7
  166.2 2.9 divide_convert_fusion.1
  171.5 2.4 collective-permute-done.1
  175.9 3.2 add_convert_fusion.2
  179.4 8.0 %fusion.39 = f32[768,2048]{1,0:T(8,128)S(1)} fusion(bf16[768,1536]{1,0:T(8,128)(2,1)} %add_convert_fusion.2, bf16[1536,2048]{1,0:T(8,128)(2,1)} %reshape.177), kind=kOutput, calls=%fused_computation.92 | convolution fusion | flops 4831838208 | bytes 14942208 | tf_op jit(solution)/shard_map/dot_general | solution.py:318
  187.4 6.7 %broadcast_select_fusion.3 = (f32[768,2048]{1,0:T(8,128)S(1)}, f32[768,2048]{1,0:T(8,128)S(1)}) fusion(f32[768,2048]{1,0:T(8,128)S(1)} %fusion.39, pred[]{:T(512)S(6)} %eq.24, bf16[768,1536]{1,0:T(8,128)(2,1)} %collective-permute-done.2, bf16[1536,2048]{1,0:T(8,128)(2,1)S(1)} %bitcast.41), kind=kOutput, calls=%fused_computation.32 | convolution fusion | flops 4834983936 | bytes 27525120 | tf_op jit(solution)/shard_map/dot_general | solution.py:320
  194.1 6.7 %pad_maximum_fusion = (f32[1536,2048]{1,0:T(8,128)}, bf16[1536,2048]{1,0:T(8,128)(2,1)S(1)}) fusion(f32[768,2048]{1,0:T(8,128)S(1)} %get-tuple-element.29, f32[768,2048]{1,0:T(8,128)S(1)} %get-tuple-element.28, f32[]{:T(128)S(6)} %sqrt.13, bf16[1536,2048]{1,0:T(8,128)(2,1)S(1)} %bitcast.41), kind=kLoop, calls=%fused_computation.6 | loop fusion | flops 18874368 | bytes 37748740 | tf_op jit(solution)/shard_map/concatenate | solution.py:322
  200.9 6.7 %fusion.2 = f32[768,1536]{1,0:T(8,128)} fusion(bf16[1536,2048]{1,0:T(8,128)(2,1)S(1)} %get-tuple-element.25, s32[]{:T(128)S(6)} %select_n.93), kind=kOutput, calls=%fused_computation.21 | convolution fusion | flops 4831838208 | bytes 14155780 | tf_op jit(solution)/shard_map/rc,sc->rs/dot_general | solution.py:288
  208.2 11.7 %convert_multiply_fusion = f32[64,2,12,2048]{3,2,1,0:T(8,128)} fusion(bf16[64,2,12,2048]{3,2,1,0:T(8,128)(2,1)} %shard_map.239), kind=kLoop, calls=%fused_computation.5 | loop fusion | flops 6291456 | bytes 18874368 | tf_op jit(solution)/shard_map/mul | solution.py:329
  219.9 5.1 fusion.4
  225.0 3.2 add_convert_fusion.1
  228.9 17.6 %copy.39 = f32[64,2,12,2048]{3,0,2,1:T(8,128)} copy(f32[64,2,12,2048]{3,2,1,0:T(8,128)} %convert_multiply_fusion) | data formatting | bytes 25165824 | tf_op jit(solution)/shard_map/mul | solution.py:329
  250.1 3.7 fusion.10
  253.9 3.0 add_convert_fusion
  259.8 9.7 %fusion.40 = f32[768,2048]{1,0:T(8,128)} fusion(bf16[768,1536]{1,0:T(8,128)(2,1)} %add_convert_fusion, bf16[1536,2048]{1,0:T(8,128)(2,1)} %copy-done), kind=kOutput, calls=%fused_computation.93 | convolution fusion | flops 4831838208 | bytes 14942208 | tf_op jit(solution)/shard_map/dot_general | solution.py:318
  269.6 8.6 %fusion.41 = f32[768,2048]{1,0:T(8,128)} fusion(bf16[768,1536]{1,0:T(8,128)(2,1)} %collective-permute-done.5, bf16[1536,2048]{1,0:T(8,128)(2,1)S(1)} %bitcast.43), kind=kOutput, calls=%fused_computation.94 | convolution fusion | flops 4831838208 | bytes 14942208 | tf_op jit(solution)/shard_map/dot_general | solution.py:320
  278.1 11.9 %broadcast_select_fusion.1 = (f32[768,2048]{1,0:T(8,128)}, f32[768,2048]{1,0:T(8,128)}) fusion(f32[768,2048]{1,0:T(8,128)} %fusion.40, f32[768,2048]{1,0:T(8,128)} %fusion.41, pred[]{:T(512)S(6)} %eq.24), kind=kLoop, calls=%fused_computation.30 | loop fusion | flops 3145728 | bytes 25165824 | tf_op jit(solution)/shard_map/jit(_where)/select_n | solution.py:324
  290.1 11.3 %pad_maximum_fusion.1 = f32[1536,2048]{1,0:T(8,128)} fusion(f32[768,2048]{1,0:T(8,128)} %get-tuple-element.27, f32[768,2048]{1,0:T(8,128)} %get-tuple-element.26), kind=kLoop, calls=%fused_computation.7 | loop fusion | flops 3145728 | bytes 25165824 | tf_op jit(solution)/shard_map/concatenate | solution.py:322
  301.4 16.1 %multiply_convert_fusion = bf16[64,24,2048]{2,1,0:T(8,128)(2,1)S(1)} fusion(f32[64,24,2048]{2,1,0:T(8,128)} %bitcast.37, f32[64,24,2048]{2,1,0:T(8,128)} %bitcast.35, f32[64,24,2048]{2,0,1:T(8,128)} %bitcast.36, f32[]{:T(128)S(6)} %sqrt.13, f32[]{:T(128)S(6)} %select_n.90), kind=kLoop, calls=%fused_computation.11 | loop fusion | flops 25165824 | bytes 44040200 | tf_op jit(solution)/shard_map/convert_element_type | solution.py:331
  317.5 4.6 pad_maximum_fusion.2.refs_0_
  322.1 191.4 %shard_map.240 = (bf16[32,25,768]{2,1,0:T(8,128)(2,1)}, bf16[24,25,2048]{2,1,0:T(8,128)(2,1)}) custom-call(bf16[64,25,2048]{2,1,0:T(8,128)(2,1)} %pad_maximum_fusion.2.refs_0_), custom_call_target="tpu_custom_call" | custom-call | tf_op jit(solution)/shard_map/pallas_call | solution.py:403
  515.3 2.6 gather_fusion.1
  519.5 2.1 gather_fusion
  (90 shorter events, 20.6 us)
Async XLA Ops:
  146.7 9.4 %collective-permute-start = (f32[768,1536]{1,0:T(8,128)}, f32[768,1536]{1,0:T(8,128)}, u32[]{:S(2)}, u32[]{:S(2)}) collective-permute-start(f32[768,1536]{1,0:T(8,128)} %fusion.6), channel_id=1, source_target_pairs={{0,1},{1,0},{2,3},{3,2},{4,5},{5,4},{6,7},{7,6},{8,9},{9,8},{10,11... | collective-permute-start | bytes 14155784 | tf_op jit(solution)/shard_map/ppermute | solution.py:273
  169.1 4.8 collective-permute-start.1
  169.5 6.4 %slice-start = ((s8[4718592]{0:T(1024)(128)(4,1)}), s8[4194304]{0:T(1024)(128)(4,1)S(1)}, s32[]{:S(2)}) async-start(s8[4718592]{0:T(1024)(128)(4,1)} %bitcast.38), calls=%async_computation | async-start | bytes 8388608
  171.5 4.4 slice-start.1
  175.9 11.5 %slice-start.2 = ((s8[6291456]{0:T(1024)(128)(4,1)}), s8[2097152]{0:T(1024)(128)(4,1)S(1)}, s32[]{:S(2)}) async-start(s8[6291456]{0:T(1024)(128)(4,1)} %bitcast.40), calls=%async_computation.2 | async-start | bytes 4194304
  179.2 8.2 %collective-permute-start.2 = (bf16[768,1536]{1,0:T(8,128)(2,1)}, bf16[768,1536]{1,0:T(8,128)(2,1)}, u32[]{:S(2)}, u32[]{:S(2)}) collective-permute-start(bf16[768,1536]{1,0:T(8,128)(2,1)} %add_convert_fusion.2), channel_id=1, source_target_pairs={{0,1},{1,0},{2,3},{3,2},{4,5},{5,4},{6,7},{7,6},{8,9},{9,8},{10,11... | collective-permute-start | bytes 7077896 | tf_op jit(solution)/shard_map/ppermute | solution.py:273
  179.4 8.0 %slice-start.3 = ((s8[6291456]{0:T(1024)(128)(4,1)}), s8[4194304]{0:T(1024)(128)(4,1)S(1)}, s32[]{:S(2)}) async-start(s8[6291456]{0:T(1024)(128)(4,1)} %bitcast.40), calls=%async_computation.3 | async-start | bytes 8388608
  200.9 6.7 %copy-start = (bf16[1536,2048]{1,0:T(8,128)(2,1)}, bf16[1536,2048]{1,0:T(8,128)(2,1)S(1)}, u32[]{:S(2)}) copy-start(bf16[1536,2048]{1,0:T(8,128)(2,1)S(1)} %get-tuple-element.25) | copy-start | bytes 18874372
  207.6 17.4 %collective-permute-start.3 = (f32[768,1536]{1,0:T(8,128)}, f32[768,1536]{1,0:T(8,128)}, u32[]{:S(2)}, u32[]{:S(2)}) collective-permute-start(f32[768,1536]{1,0:T(8,128)} %fusion.2), channel_id=1, source_target_pairs={{0,1},{1,0},{2,3},{3,2},{4,5},{5,4},{6,7},{7,6},{8,9},{9,8},{10,11... | collective-permute-start | bytes 14155784 | tf_op jit(solution)/shard_map/ppermute | solution.py:273
  208.2 11.7 %copy-start.1 = (bf16[1536,2048]{1,0:T(8,128)(2,1)S(1)}, bf16[1536,2048]{1,0:T(8,128)(2,1)}, u32[]{:S(2)}) copy-start(bf16[1536,2048]{1,0:T(8,128)(2,1)} %copy-done) | copy-start | bytes 18874372
  225.0 3.9 copy-start.12
  228.3 21.9 %collective-permute-start.4 = (bf16[768,1536]{1,0:T(8,128)(2,1)S(1)}, bf16[768,1536]{1,0:T(8,128)(2,1)}, u32[]{:S(2)}, u32[]{:S(2)}) collective-permute-start(bf16[768,1536]{1,0:T(8,128)(2,1)S(1)} %add_convert_fusion.1), channel_id=1, source_target_pairs={{0,1},{1,0},{2,3},{3,2},{4,5},{5,4},{6,7},{7,6},{8,9},{9,8},{10,11... | collective-permute-start | bytes 7077896 | tf_op jit(solution)/shard_map/ppermute | solution.py:273
  228.9 18.2 %copy-start.13 = (s32[32]{0:T(128)S(1)}, s32[32]{0:T(128)}, u32[]{:S(2)}) copy-start(s32[32]{0:T(128)} %param.20) | copy-start | bytes 388
  228.9 19.1 %copy-start.10 = (s32[16,2]{0,1:T(2,128)S(1)}, s32[16,2]{0,1:T(2,128)}, u32[]{:S(2)}) copy-start(s32[16,2]{0,1:T(2,128)} %param.31) | copy-start | bytes 388
  253.8 3.6 copy-start.6
  253.8 3.6 copy-start.7
  253.8 3.6 copy-start.8
  253.8 3.6 copy-start.9
  253.9 4.2 copy-start.2
  253.9 4.2 copy-start.3
  253.9 4.2 copy-start.4
  253.9 4.2 copy-start.5
  256.9 12.7 %collective-permute-start.5 = (bf16[768,1536]{1,0:T(8,128)(2,1)}, bf16[768,1536]{1,0:T(8,128)(2,1)}, u32[]{:S(2)}, u32[]{:S(2)}) collective-permute-start(bf16[768,1536]{1,0:T(8,128)(2,1)} %add_convert_fusion), channel_id=1, source_target_pairs={{0,1},{1,0},{2,3},{3,2},{4,5},{5,4},{6,7},{7,6},{8,9},{9,8},{10,11... | collective-permute-start | bytes 7077896 | tf_op jit(solution)/shard_map/ppermute | solution.py:273
  258.1 11.4 %slice-start.4 = ((s8[6291456]{0:T(1024)(128)(4,1)}), s8[2097152]{0:T(1024)(128)(4,1)S(1)}, s32[]{:S(2)}) async-start(s8[6291456]{0:T(1024)(128)(4,1)} %bitcast.42), calls=%async_computation.4 | async-start | bytes 4194304
  259.8 9.7 %slice-start.5 = ((s8[6291456]{0:T(1024)(128)(4,1)}), s8[4194304]{0:T(1024)(128)(4,1)S(1)}, s32[]{:S(2)}) async-start(s8[6291456]{0:T(1024)(128)(4,1)} %bitcast.42), calls=%async_computation.5 | async-start | bytes 8388608
  518.0 5.6 %copy-start.11 = (s32[56]{0:T(128)S(1)}, s32[56]{0:T(128)}, u32[]{:S(2)}) copy-start(s32[56]{0:T(128)} %param.22) | copy-start | bytes 676

commit v6 on v5

--- a/solution.py
+++ b/solution.py
@@ -318,19 +318,19 @@
             jnp.dot(polynomial, current, preferred_element_type=jnp.float32)
         )
         product_other = jnp.dot(poly_other, current, preferred_element_type=jnp.float32)
-        first = t == 0
-        product = jnp.concatenate(
-            [
-                jnp.where(first, product_mine, product_other),
-                jnp.where(first, product_other, product_mine),
-            ],
-            axis=0,
-        )
-        mixed = (QUINTIC_LINEAR * current.astype(jnp.float32) + product) / jnp.sqrt(gram_scale)
-        if round_index == NS_STEPS - 1:
-            iterate = (factor * mixed).astype(jnp.bfloat16)
-        else:
-            iterate = mixed.astype(jnp.bfloat16)
+        scale_root = jnp.sqrt(gram_scale)
+        halves = []
+        for rows_here, product_here in ((my_rows, product_mine), (their_rows, product_other)):
+            mixed = (QUINTIC_LINEAR * rows_here.astype(jnp.float32) + product_here) / scale_root
+            if round_index == NS_STEPS - 1:
+                mixed = factor * mixed
+            halves.append(mixed.astype(jnp.bfloat16))
+        iterate = lax.dynamic_update_slice_in_dim(
+            lax.dynamic_update_slice_in_dim(jnp.zeros_like(current), halves[0], mine, 0),
+            halves[1],
+            theirs,
+            0,
+        )
     return (iterate, first_scale)
 
 

time: 532 us -> 465 us (0.87)
  other arithmetic: 96.8 us -> 48.7 us
  local copies, waits for them, and re-layouts: 47.5 us -> 33 us
    concatenate x2 -> x0, other arithmetic: 18 us -> none  [orthogonalize(): jnp.concatenate([jnp.where(first, product_mine, product_other), jnp.where...]
    mul x1 -> x0, local copies, waits for them, and re-layouts: 17.6 us -> none  [orthogonalize(): QUINTIC_LINEAR * current.astype(jnp.float32) + product]
    convert_element_type x1 -> x0, other arithmetic: 16.1 us -> none  [orthogonalize(): iterate = (factor * mixed).astype(jnp.bfloat16)]
    select_n x1 -> x0, other arithmetic: 11.9 us -> none  [orthogonalize(): jnp.where(first, product_mine, product_other)]
    mul x1 -> x0, other arithmetic: 11.7 us -> none  [orthogonalize(): QUINTIC_LINEAR * current.astype(jnp.float32) + product]
  transfers between devices with their start and end apart: 6 -> 6, of which waited for: 1 -> 1; matrix products, arithmetic and copies ran while one was open for 13% -> 12% of each run, Pallas kernels for 0% -> 0%
where the time goes in v6:
time: 465 us; the launch traced here: 457 us
  Pallas kernels  294 us (63%)
  matrix products  70.9 us (15%)
  other arithmetic  48.7 us (10%)
  local copies, waits for them, and re-layouts  33 us (7%)
    pallas_call x1, Pallas kernels, local(): pl.pallas_call(lambda *refs: gather_kernel(n_sq, n_sw, *refs), out_shape=...  189 us
    pallas_call x1, Pallas kernels, local(): pl.pallas_call(lambda *refs: scatter_kernel(n_sq, n_sw, *refs), out_shape...  105 us
    dot_general x2, matrix products, orthogonalize(): jnp.einsum('rc,sc->rs', my_rows, current, preferred_element_type=jnp.floa...  17.7 us
    dot_general x2, matrix products, orthogonalize(): jnp.einsum('rc,sc->rs', their_rows, current, preferred_element_type=jnp.f...  16.4 us
    dot_general x2, matrix products, orthogonalize(): jnp.dot(polynomial, current, preferred_element_type=jnp.float32)  14.8 us
    dot_general x2, matrix products, orthogonalize(): jnp.dot(poly_other, current, preferred_element_type=jnp.float32)  12.2 us
    convert_element_type x2, other arithmetic, momentum_terms(): return (state_next, (gradient + MOMENTUM * state_next).astype(jnp.bfloat16))  10.9 us
    reshape x1, local copies, waits for them, and re-layouts, local(): iterate, first_scale = orthogonalize(arrived.reshape(D, half), factor)  10.7 us
  transfers between devices with their start and end apart: 6, of which 1 were waited for; matrix products, arithmetic and copies ran while one was open for 12% of the time, Pallas kernels for 0%

profile of v6, /device:TPU:64, one launch (start us, length us, event | category | flops | bytes accessed | tf_op | source)
XLA Modules:
  0.0 456.7 jit_solution(11613711018307079936)
XLA Ops:
  0.6 6.7 %add_convert_fusion.3 = (bf16[24,49152]{1,0:T(8,128)(2,1)S(1)}, f32[24,49152]{1,0:T(8,128)}) fusion(f32[24,49152]{1,0:T(8,128)} %param.18, f32[24,49152]{1,0:T(8,128)} %param.19), kind=kLoop, calls=%fused_computation.15 | loop fusion | flops 5898240 | bytes 16515072 | tf_op jit(solution)/shard_map/convert_element_type | solution.py:25
  7.4 3.2 reshape.172.refs_1_
  10.6 4.2 add_convert_fusion.4
  14.8 1.8 reshape.171.refs_0_
  16.5 4.4 broadcast_in_dim.58.clone.refs_2_
  20.9 105.4 %shard_map.239 = bf16[64,2,12,2048]{3,2,1,0:T(8,128)(2,1)} custom-call(bf16[32,12,1536]{2,1,0:T(8,128)(2,1)} %reshape.171.refs_0_, bf16[24,12,4096]{2,1,0:T(8,128)(2,1)} %reshape.172.refs_1_, bf16[64,2,12,2048]{3,2,1,0:T(8,128)(2,1)} %broadcast_in_dim.58.clone.refs_2_), custom_call_target="tpu_custom_call", output_to_operand_aliasing={{}: (2, {})} | custom-call | tf_op jit(solution)/shard_map/pallas_call | solution.py:382
  126.3 10.7 %reshape.173 = bf16[1536,2048]{1,0:T(8,128)(2,1)} reshape(bf16[64,2,12,2048]{3,2,1,0:T(8,128)(2,1)} %shard_map.239) | data formatting | bytes 12582912 | tf_op jit(solution)/shard_map/reshape | solution.py:401
  137.0 9.6 %fusion.8 = f32[768,1536]{1,0:T(8,128)} fusion(bf16[1536,2048]{1,0:T(8,128)(2,1)} %reshape.173, s32[]{:T(128)S(6)} %select_n.76), kind=kOutput, calls=%fused_computation.25 | convolution fusion | flops 4831838208 | bytes 14155780 | tf_op jit(solution)/shard_map/rc,sc->rs/dot_general | solution.py:288
  147.1 8.8 %fusion.10 = f32[768,1536]{1,0:T(8,128)S(1)} fusion(bf16[1536,2048]{1,0:T(8,128)(2,1)} %reshape.173, s32[]{:T(128)S(6)} %select_n.75), kind=kOutput, calls=%fused_computation.27 | convolution fusion | flops 4831838208 | bytes 14155780 | tf_op jit(solution)/shard_map/rc,sc->rs/dot_general | solution.py:291
  156.0 6.4 %multiply_reduce_fusion = (f32[]{:T(128)}, f32[768,1536]{1,0:T(8,128)}) fusion(f32[768,1536]{1,0:T(8,128)S(1)} %fusion.10, f32[768,1536]{1,0:T(8,128)} %collective-permute-done), kind=kLoop, calls=%fused_computation.14 | loop fusion | flops 3538943 | bytes 14155780 | tf_op jit(solution)/shard_map/reduce_sum | solution.py:295
  162.3 3.1 psum.7
  166.1 2.9 divide_convert_fusion.2
  169.7 2.0 fusion.18
  171.7 2.4 collective-permute-done.1
  174.1 2.0 fusion.16
  176.1 3.2 add_convert_fusion.2
  179.6 8.0 %fusion.41 = f32[768,2048]{1,0:T(8,128)S(1)} fusion(bf16[768,1536]{1,0:T(8,128)(2,1)} %add_convert_fusion.2, bf16[1536,2048]{1,0:T(8,128)(2,1)} %reshape.173), kind=kOutput, calls=%fused_computation.88 | convolution fusion | flops 4831838208 | bytes 14942208 | tf_op jit(solution)/shard_map/dot_general | solution.py:318
  190.0 6.9 %fusion.1 = bf16[1536,2048]{1,0:T(8,128)(2,1)S(1)} fusion(bf16[1536,2048]{1,0:T(8,128)(2,1)S(1)} %fusion.2, s32[]{:T(128)S(6)} %select_n.76, bf16[768,1536]{1,0:T(8,128)(2,1)} %collective-permute-done.2, bf16[1536,2048]{1,0:T(8,128)(2,1)S(1)} %bitcast.37, f32[]{:T(128)S(6)} %sqrt.13), kind=kOutput, calls=%fused_computation.18 | convolution fusion | flops 4839702528 | bytes 14942216 | tf_op jit(solution)/shard_map/dot_general | solution.py:320
  197.0 6.8 %fusion.4 = f32[768,1536]{1,0:T(8,128)} fusion(bf16[1536,2048]{1,0:T(8,128)(2,1)S(1)} %fusion.1, s32[]{:T(128)S(6)} %select_n.76), kind=kOutput, calls=%fused_computation.21 | convolution fusion | flops 4831838208 | bytes 14155780 | tf_op jit(solution)/shard_map/rc,sc->rs/dot_general | solution.py:288
  206.1 8.9 %fusion.6 = f32[768,1536]{1,0:T(8,128)S(1)} fusion(bf16[1536,2048]{1,0:T(8,128)(2,1)} %copy-done, s32[]{:T(128)S(6)} %select_n.75), kind=kOutput, calls=%fused_computation.23 | convolution fusion | flops 4831838208 | bytes 14155780 | tf_op jit(solution)/shard_map/rc,sc->rs/dot_general | solution.py:291
  215.0 3.3 add_convert_fusion.1
  225.7 2.4 fusion.22
  228.1 2.0 fusion.14
  230.2 3.8 fusion.12
  234.0 3.0 add_convert_fusion
  237.9 6.8 %fusion.42 = f32[768,2048]{1,0:T(8,128)S(1)} fusion(bf16[768,1536]{1,0:T(8,128)(2,1)} %add_convert_fusion, bf16[1536,2048]{1,0:T(8,128)(2,1)S(1)} %bitcast.39), kind=kOutput, calls=%fused_computation.89 | convolution fusion | flops 4831838208 | bytes 14942208 | tf_op jit(solution)/shard_map/dot_general | solution.py:318
  245.5 1.6 fusion.3
  247.1 5.3 %fusion = bf16[1536,2048]{1,0:T(8,128)(2,1)S(1)} fusion(bf16[1536,2048]{1,0:T(8,128)(2,1)S(1)} %fusion.3, s32[]{:T(128)S(6)} %select_n.76, bf16[768,1536]{1,0:T(8,128)(2,1)S(1)} %collective-permute-done.5, bf16[1536,2048]{1,0:T(8,128)(2,1)S(1)} %bitcast.39, f32[]{:T(128)S(6)} %select_n.74), kind=kOutput, calls=%fused_computation.17 | convolution fusion | flops 4839702528 | bytes 14942216 | tf_op jit(solution)/shard_map/dot_general | solution.py:320
  252.4 4.5 pad_maximum_fusion.refs_0_
  256.9 188.6 %shard_map.240 = (bf16[32,25,768]{2,1,0:T(8,128)(2,1)}, bf16[24,25,2048]{2,1,0:T(8,128)(2,1)}) custom-call(bf16[64,25,2048]{2,1,0:T(8,128)(2,1)} %pad_maximum_fusion.refs_0_), custom_call_target="tpu_custom_call" | custom-call | tf_op jit(solution)/shard_map/pallas_call | solution.py:403
  447.4 2.6 gather_fusion.1
  451.6 2.2 gather_fusion
  (78 shorter events, 21.2 us)
Async XLA Ops:
  146.6 9.3 %collective-permute-start = (f32[768,1536]{1,0:T(8,128)}, f32[768,1536]{1,0:T(8,128)}, u32[]{:S(2)}, u32[]{:S(2)}) collective-permute-start(f32[768,1536]{1,0:T(8,128)} %fusion.8), channel_id=1, source_target_pairs={{0,1},{1,0},{2,3},{3,2},{4,5},{5,4},{6,7},{7,6},{8,9},{9,8},{10,11... | collective-permute-start | bytes 14155784 | tf_op jit(solution)/shard_map/ppermute | solution.py:273
  169.0 5.1 %collective-permute-start.1 = (bf16[768,1536]{1,0:T(8,128)(2,1)S(1)}, bf16[768,1536]{1,0:T(8,128)(2,1)S(1)}, u32[]{:S(2)}, u32[]{:S(2)}) collective-permute-start(bf16[768,1536]{1,0:T(8,128)(2,1)S(1)} %divide_convert_fusion.2), channel_id=1, source_target_pairs={{0,1},{1,0},{2,3},{3,2},{4,5},{5,4},{6,7},{7,6},{8,9},{9,8},{10,11... | collective-permute-start | bytes 7077896 | tf_op jit(solution)/shard_map/ppermute | solution.py:273
  169.7 6.4 %slice-start = ((s8[4718592]{0:T(1024)(128)(4,1)}), s8[4194304]{0:T(1024)(128)(4,1)S(1)}, s32[]{:S(2)}) async-start(s8[4718592]{0:T(1024)(128)(4,1)} %bitcast.33), calls=%async_computation | async-start | bytes 8388608
  171.7 4.4 slice-start.1
  176.1 12.3 %slice-start.2 = ((s8[6291456]{0:T(1024)(128)(4,1)}), s8[2097152]{0:T(1024)(128)(4,1)S(1)}, s32[]{:S(2)}) async-start(s8[6291456]{0:T(1024)(128)(4,1)} %bitcast.36), calls=%async_computation.2 | async-start | bytes 4194304
  179.3 10.7 %collective-permute-start.2 = (bf16[768,1536]{1,0:T(8,128)(2,1)}, bf16[768,1536]{1,0:T(8,128)(2,1)}, u32[]{:S(2)}, u32[]{:S(2)}) collective-permute-start(bf16[768,1536]{1,0:T(8,128)(2,1)} %add_convert_fusion.2), channel_id=1, source_target_pairs={{0,1},{1,0},{2,3},{3,2},{4,5},{5,4},{6,7},{7,6},{8,9},{9,8},{10,11... | collective-permute-start | bytes 7077896 | tf_op jit(solution)/shard_map/ppermute | solution.py:273
  179.6 8.8 %slice-start.3 = ((s8[6291456]{0:T(1024)(128)(4,1)}), s8[4194304]{0:T(1024)(128)(4,1)S(1)}, s32[]{:S(2)}) async-start(s8[6291456]{0:T(1024)(128)(4,1)} %bitcast.36), calls=%async_computation.3 | async-start | bytes 8388608
  197.0 6.9 %copy-start = (bf16[1536,2048]{1,0:T(8,128)(2,1)}, bf16[1536,2048]{1,0:T(8,128)(2,1)S(1)}, u32[]{:S(2)}) copy-start(bf16[1536,2048]{1,0:T(8,128)(2,1)S(1)} %fusion.1) | copy-start | bytes 18874372
  197.0 7.4 %copy-start.6 = (s32[24]{0:T(128)S(1)}, s32[24]{0:T(128)}, u32[]{:S(2)}) copy-start(s32[24]{0:T(128)} %param.21) | copy-start | bytes 292
  197.0 8.6 %copy-start.7 = (s32[32]{0:T(128)S(1)}, s32[32]{0:T(128)}, u32[]{:S(2)}) copy-start(s32[32]{0:T(128)} %param.20) | copy-start | bytes 388
  203.8 11.2 %collective-permute-start.3 = (f32[768,1536]{1,0:T(8,128)}, f32[768,1536]{1,0:T(8,128)}, u32[]{:S(2)}, u32[]{:S(2)}) collective-permute-start(f32[768,1536]{1,0:T(8,128)} %fusion.4), channel_id=1, source_target_pairs={{0,1},{1,0},{2,3},{3,2},{4,5},{5,4},{6,7},{7,6},{8,9},{9,8},{10,11... | collective-permute-start | bytes 14155784 | tf_op jit(solution)/shard_map/ppermute | solution.py:273
  214.9 9.4 %copy-start.4 = (f32[1344]{0:T(1024)S(1)}, f32[1344]{0:T(1024)}, u32[]{:S(2)}) copy-start(f32[1344]{0:T(1024)} %param.23) | copy-start | bytes 16132
  214.9 10.8 %copy-start.1 = (f32[128,768]{1,0:T(8,128)S(1)}, f32[128,768]{1,0:T(8,128)}, u32[]{:S(2)}) copy-start(f32[128,768]{1,0:T(8,128)} %param.30) | copy-start | bytes 1179652
  215.0 10.8 %copy-start.2 = (f32[128,768]{1,0:T(8,128)S(1)}, f32[128,768]{1,0:T(8,128)}, u32[]{:S(2)}) copy-start(f32[128,768]{1,0:T(8,128)} %param.28) | copy-start | bytes 1179652
  215.0 10.8 %copy-start.3 = (f32[128,768]{1,0:T(8,128)S(1)}, f32[128,768]{1,0:T(8,128)}, u32[]{:S(2)}) copy-start(f32[128,768]{1,0:T(8,128)} %param.27) | copy-start | bytes 1179652
  218.3 11.8 %collective-permute-start.4 = (bf16[768,1536]{1,0:T(8,128)(2,1)S(1)}, bf16[768,1536]{1,0:T(8,128)(2,1)}, u32[]{:S(2)}, u32[]{:S(2)}) collective-permute-start(bf16[768,1536]{1,0:T(8,128)(2,1)S(1)} %add_convert_fusion.1), channel_id=1, source_target_pairs={{0,1},{1,0},{2,3},{3,2},{4,5},{5,4},{6,7},{7,6},{8,9},{9,8},{10,11... | collective-permute-start | bytes 7077896 | tf_op jit(solution)/shard_map/ppermute | solution.py:273
  220.2 0.7 copy-start.8
  230.1 7.8 %slice-start.4 = ((s8[6291456]{0:T(1024)(128)(4,1)}), s8[4194304]{0:T(1024)(128)(4,1)S(1)}, s32[]{:S(2)}) async-start(s8[6291456]{0:T(1024)(128)(4,1)} %bitcast.38), calls=%async_computation.4 | async-start | bytes 8388608
  234.0 3.9 slice-start.5
  236.9 10.2 %collective-permute-start.5 = (bf16[768,1536]{1,0:T(8,128)(2,1)}, bf16[768,1536]{1,0:T(8,128)(2,1)S(1)}, u32[]{:S(2)}, u32[]{:S(2)}) collective-permute-start(bf16[768,1536]{1,0:T(8,128)(2,1)} %add_convert_fusion), channel_id=1, source_target_pairs={{0,1},{1,0},{2,3},{3,2},{4,5},{5,4},{6,7},{7,6},{8,9},{9,8},{10,11... | collective-permute-start | bytes 7077896 | tf_op jit(solution)/shard_map/ppermute | solution.py:273
  450.1 5.8 %copy-start.5 = (s32[56]{0:T(128)S(1)}, s32[56]{0:T(128)}, u32[]{:S(2)}) copy-start(s32[56]{0:T(128)} %param.22) | copy-start | bytes 676

commit v7 on v6

--- a/solution.py
+++ b/solution.py
@@ -379,26 +379,23 @@
     sw_pieces = swiglu_send.reshape(n_sw, flat_rows, FF)
 
     half = FF // 2
-    arrived = pl.pallas_call(
-        lambda *refs: scatter_kernel(n_sq, n_sw, *refs),
-        out_shape=jax.ShapeDtypeStruct((wide_count, 2, flat_rows, half), jnp.bfloat16),
-        in_specs=[pl.BlockSpec(memory_space=pl.ANY)] * 3,
-        out_specs=pl.BlockSpec(memory_space=pl.ANY),
-        scratch_shapes=[
-            pltpu.VMEM((n_sq, 2, flat_rows, D // 2), jnp.bfloat16),
-            pltpu.VMEM((n_sw, 2, flat_rows, half), jnp.bfloat16),
-            pltpu.SemaphoreType.DMA((n_sq + n_sw,)),
-            pltpu.SemaphoreType.DMA((1,)),
-            pltpu.SemaphoreType.DMA((6,)),
-        ],
-        input_output_aliases={2: 0},
-        compiler_params=pltpu.CompilerParams(collective_id=0, has_side_effects=True),
-    )(sq_pieces, sw_pieces, jnp.zeros((wide_count, 2, flat_rows, half), jnp.bfloat16))
+    sq_halves = jnp.pad(
+        sq_pieces.reshape(n_sq, flat_rows, 2, D // 2).transpose(0, 2, 1, 3),
+        ((0, 0), (0, 0), (0, 0), (0, half - D // 2)),
+    )
+    sw_halves = sw_pieces.reshape(n_sw, flat_rows, 2, half).transpose(0, 2, 1, 3)
+    outgoing = jnp.pad(
+        jnp.concatenate([sq_halves, sw_halves], axis=0),
+        ((0, wide_count - n_sq - n_sw), (0, 0), (0, 0), (0, 0)),
+    )
+    arrived = lax.all_to_all(
+        outgoing.reshape(D, half), ("dp", "tensor"), split_axis=0, concat_axis=0, tiled=True
+    )
 
     is_sq = d < n_sq
     is_sw = (d >= n_sq) & (d < n_sq + n_sw)
     factor = jnp.where(is_sq, jnp.float32(math.sqrt(D)), jnp.float32(math.sqrt(FF)))
-    iterate, first_scale = orthogonalize(arrived.reshape(D, half), factor)
+    iterate, first_scale = orthogonalize(arrived, factor)
 
     returned_sq, returned_sw = pl.pallas_call(
         lambda *refs: gather_kernel(n_sq, n_sw, *refs),

time: 465 us -> 440 us (0.946)
  Pallas kernels: 294 us -> 151 us
  waiting for transfers between devices: 2.38 us -> 98.5 us
  starting transfers between devices: 2.67 us -> 13 us
  other arithmetic: 48.7 us -> 55.7 us
    pallas_call x1 -> x0, Pallas kernels: 105 us -> none  [local(): pl.pallas_call(lambda *refs: scatter_kernel(n_sq, n_sw, *refs), out_shape...]
    all_to_all x0 -> x1, waiting for transfers between devices: none -> 96.1 us  [local(): lax.all_to_all(outgoing.reshape(D, half), ('dp', 'tensor'), split_axis=0,...]
    pallas_call x1, Pallas kernels: 189 us -> 151 us  [local(): pl.pallas_call(lambda *refs: gather_kernel(n_sq, n_sw, *refs), out_shape=...]
    reshape x3 -> x0, local copies, waits for them, and re-layouts: 15.7 us -> none  [the longest x1 10.7 us: local(): iterate, first_scale = orthogonalize(arrived.reshape(D, half), factor)]
    all_to_all x0 -> x1, local copies, waits for them, and re-layouts: none -> 10.7 us  [local(): lax.all_to_all(outgoing.reshape(D, half), ('dp', 'tensor'), split_axis=0,...]
    all_to_all x0 -> x1, starting transfers between devices: none -> 10.5 us  [local(): lax.all_to_all(outgoing.reshape(D, half), ('dp', 'tensor'), split_axis=0,...]
    concatenate x0 -> x1, other arithmetic: none -> 5.92 us  [local(): jnp.concatenate([sq_halves, sw_halves], axis=0)]
    another operation x2 -> x4, local copies, waits for them, and re-layouts: 1.57 us -> 7.04 us  [the longest x1 3.53 us: local(): sw_pieces.reshape(n_sw, flat_rows, 2, half).transpose(0, 2, 1, 3)]
  transfers between devices with their start and end apart: 6 -> 7, of which waited for: 1 -> 2; matrix products, arithmetic and copies ran while one was open for 12% -> 12% of each run, Pallas kernels for 0% -> 0%
where the time goes in v7:
time: 440 us; the launch traced here: 432 us
  Pallas kernels  151 us (34%)
  waiting for transfers between devices  98.5 us (22%)
  matrix products  71 us (16%)
  other arithmetic  55.7 us (13%)
  local copies, waits for them, and re-layouts  37.1 us (8%)
  starting transfers between devices  13 us (3%)
    pallas_call x1, Pallas kernels, local(): pl.pallas_call(lambda *refs: gather_kernel(n_sq, n_sw, *refs), out_shape=...  151 us
    all_to_all x1, waiting for transfers between devices, local(): lax.all_to_all(outgoing.reshape(D, half), ('dp', 'tensor'), split_axis=0,...  96.1 us
    dot_general x2, matrix products, orthogonalize(): jnp.einsum('rc,sc->rs', my_rows, current, preferred_element_type=jnp.floa...  17.9 us
    dot_general x2, matrix products, orthogonalize(): jnp.einsum('rc,sc->rs', their_rows, current, preferred_element_type=jnp.f...  16.3 us
    dot_general x2, matrix products, orthogonalize(): jnp.dot(polynomial, current, preferred_element_type=jnp.float32)  14.8 us
    dot_general x2, matrix products, orthogonalize(): jnp.dot(poly_other, current, preferred_element_type=jnp.float32)  12.2 us
    convert_element_type x2, other arithmetic, momentum_terms(): return (state_next, (gradient + MOMENTUM * state_next).astype(jnp.bfloat16))  12.1 us
    all_to_all x1, local copies, waits for them, and re-layouts, local(): lax.all_to_all(outgoing.reshape(D, half), ('dp', 'tensor'), split_axis=0,...  10.7 us
  transfers between devices with their start and end apart: 7, of which 2 were waited for; matrix products, arithmetic and copies ran while one was open for 12% of the time, Pallas kernels for 0%

profile of v7, /device:TPU:64, one launch (start us, length us, event | category | flops | bytes accessed | tf_op | source)
XLA Modules:
  0.0 432.0 jit_solution(5240941711291668847)
XLA Ops:
  0.6 7.5 %add_convert_fusion.3 = (bf16[24,49152]{1,0:T(8,128)(2,1)}, f32[24,49152]{1,0:T(8,128)}) fusion(f32[24,49152]{1,0:T(8,128)} %param.18, f32[24,49152]{1,0:T(8,128)} %param.19), kind=kLoop, calls=%fused_computation.17 | loop fusion | flops 5898240 | bytes 16515072 | tf_op jit(solution)/shard_map/convert_element_type | solution.py:25
  8.1 3.5 reshape_reshape.7
  11.7 4.6 %add_convert_fusion.4 = (bf16[32,18432]{1,0:T(8,128)(2,1)}, f32[32,18432]{1,0:T(8,128)}) fusion(f32[32,18432]{1,0:T(8,128)} %param.16, f32[32,18432]{1,0:T(8,128)} %param.17), kind=kLoop, calls=%fused_computation.31 | loop fusion | flops 2949120 | bytes 8257536 | tf_op jit(solution)/shard_map/convert_element_type | solution.py:25
  18.2 5.9 %fusion = bf16[56,2,12,2048]{3,1,2,0:T(2,128)(2,1)S(1)} fusion(bf16[32,2,12,768]{3,1,2,0:T(2,128)(2,1)S(1)} %bitcast.45, bf16[24,2,12,2048]{3,1,2,0:T(2,128)(2,1)S(1)} %bitcast.44), kind=kLoop, calls=%fused_computation.11 | loop fusion | flops 16515072 | bytes 9043968 | tf_op jit(solution)/shard_map/concatenate | solution.py:388
  24.1 3.0 copy.39
  27.1 4.8 %pad.9.clone = bf16[64,2,12,2048]{3,2,1,0:T(8,128)(2,1)} pad(bf16[56,2,12,2048]{3,2,1,0:T(8,128)(2,1)S(1)} %copy.39, bf16[]{:T(256)} %constant.27.clone.1), padding=0_8x0_0x0_0x0_0 | pad | bytes 11796482 | tf_op jit(solution)/shard_map/jit(_pad)/pad | solution.py:387
  31.9 10.5 %all-to-all-start = ((bf16[128,12,2048]{2,1,0:T(8,128)(2,1)}), bf16[128,12,2048]{2,1,0:T(8,128)(2,1)}, u32[]{:S(2)}, u32[]{:S(2)}) async-start(bf16[128,12,2048]{2,1,0:T(8,128)(2,1)} %bitcast.38), calls=%async_computation | async-start | bytes 16777216 | tf_op jit(solution)/shard_map/all_to_all | solution.py:391
  42.4 96.1 %all-to-all-done = bf16[128,12,2048]{2,1,0:T(8,128)(2,1)} async-done(((bf16[128,12,2048]{2,1,0:T(8,128)(2,1)}), bf16[128,12,2048]{2,1,0:T(8,128)(2,1)}, u32[]{:S(2)}, u32[]{:S(2)}) %all-to-all-start) | async-done | bytes 6291488 | tf_op jit(solution)/shard_map/all_to_all | solution.py:391
  138.5 10.7 %all_to_all.10 = bf16[1536,2048]{1,0:T(8,128)(2,1)} reshape(bf16[128,12,2048]{2,1,0:T(8,128)(2,1)} %all-to-all-done) | data formatting | bytes 12582912 | tf_op jit(solution)/shard_map/all_to_all | solution.py:391
  149.2 9.6 %fusion.9 = f32[768,1536]{1,0:T(8,128)} fusion(bf16[1536,2048]{1,0:T(8,128)(2,1)} %all_to_all.10, s32[]{:T(128)S(6)} %select_n.76), kind=kOutput, calls=%fused_computation.27 | convolution fusion | flops 4831838208 | bytes 14155780 | tf_op jit(solution)/shard_map/rc,sc->rs/dot_general | solution.py:288
  159.8 9.1 %fusion.11 = f32[768,1536]{1,0:T(8,128)S(1)} fusion(bf16[1536,2048]{1,0:T(8,128)(2,1)} %all_to_all.10, s32[]{:T(128)S(6)} %select_n.75), kind=kOutput, calls=%fused_computation.29 | convolution fusion | flops 4831838208 | bytes 14155780 | tf_op jit(solution)/shard_map/rc,sc->rs/dot_general | solution.py:291
  168.9 6.3 %multiply_reduce_fusion = (f32[]{:T(128)}, f32[768,1536]{1,0:T(8,128)}) fusion(f32[768,1536]{1,0:T(8,128)S(1)} %fusion.11, f32[768,1536]{1,0:T(8,128)} %collective-permute-done), kind=kLoop, calls=%fused_computation.16 | loop fusion | flops 3538943 | bytes 14155780 | tf_op jit(solution)/shard_map/reduce_sum | solution.py:295
  175.2 3.1 psum.7
  179.0 2.9 divide_convert_fusion.2
  182.1 2.0 fusion.19
  184.1 2.4 collective-permute-done.1
  186.5 2.0 fusion.17
  188.5 3.2 add_convert_fusion.2
  192.1 8.0 %fusion.42 = f32[768,2048]{1,0:T(8,128)S(1)} fusion(bf16[768,1536]{1,0:T(8,128)(2,1)} %add_convert_fusion.2, bf16[1536,2048]{1,0:T(8,128)(2,1)} %all_to_all.10), kind=kOutput, calls=%fused_computation.90 | convolution fusion | flops 4831838208 | bytes 14942208 | tf_op jit(solution)/shard_map/dot_general | solution.py:318
  202.6 6.9 %fusion.2 = bf16[1536,2048]{1,0:T(8,128)(2,1)S(1)} fusion(bf16[1536,2048]{1,0:T(8,128)(2,1)S(1)} %fusion.3, s32[]{:T(128)S(6)} %select_n.76, bf16[768,1536]{1,0:T(8,128)(2,1)} %collective-permute-done.2, bf16[1536,2048]{1,0:T(8,128)(2,1)S(1)} %bitcast.41, f32[]{:T(128)S(6)} %sqrt.13), kind=kOutput, calls=%fused_computation.20 | convolution fusion | flops 4839702528 | bytes 14942216 | tf_op jit(solution)/shard_map/dot_general | solution.py:320
  209.6 6.7 %fusion.5 = f32[768,1536]{1,0:T(8,128)} fusion(bf16[1536,2048]{1,0:T(8,128)(2,1)S(1)} %fusion.2, s32[]{:T(128)S(6)} %select_n.76), kind=kOutput, calls=%fused_computation.23 | convolution fusion | flops 4831838208 | bytes 14155780 | tf_op jit(solution)/shard_map/rc,sc->rs/dot_general | solution.py:288
  218.3 8.9 %fusion.7 = f32[768,1536]{1,0:T(8,128)S(1)} fusion(bf16[1536,2048]{1,0:T(8,128)(2,1)} %copy-done, s32[]{:T(128)S(6)} %select_n.75), kind=kOutput, calls=%fused_computation.25 | convolution fusion | flops 4831838208 | bytes 14155780 | tf_op jit(solution)/shard_map/rc,sc->rs/dot_general | solution.py:291
  227.3 3.3 add_convert_fusion.1
  238.2 2.4 fusion.23
  242.6 3.8 fusion.13
  246.5 3.0 add_convert_fusion
  250.2 6.8 %fusion.43 = f32[768,2048]{1,0:T(8,128)S(1)} fusion(bf16[768,1536]{1,0:T(8,128)(2,1)} %add_convert_fusion, bf16[1536,2048]{1,0:T(8,128)(2,1)S(1)} %bitcast.43), kind=kOutput, calls=%fused_computation.91 | convolution fusion | flops 4831838208 | bytes 14942208 | tf_op jit(solution)/shard_map/dot_general | solution.py:318
  259.4 5.3 %fusion.1 = bf16[1536,2048]{1,0:T(8,128)(2,1)S(1)} fusion(bf16[1536,2048]{1,0:T(8,128)(2,1)S(1)} %fusion.4, s32[]{:T(128)S(6)} %select_n.76, bf16[768,1536]{1,0:T(8,128)(2,1)S(1)} %collective-permute-done.5, bf16[1536,2048]{1,0:T(8,128)(2,1)S(1)} %bitcast.43, f32[]{:T(128)S(6)} %select_n.74), kind=kOutput, calls=%fused_computation.19 | convolution fusion | flops 4839702528 | bytes 14942216 | tf_op jit(solution)/shard_map/dot_general | solution.py:320
  264.7 4.5 %pad_maximum_fusion.refs_0_ = bf16[64,25,2048]{2,1,0:T(8,128)(2,1)} fusion(bf16[64,1,2048]{2,1,0:T(2,128)(2,1)S(1)} %broadcast_select_fusion, bf16[64,24,2048]{2,1,0:T(8,128)(2,1)S(1)} %bitcast.39), kind=kLoop, calls=%fused_computation.6 | loop fusion | flops 13107200 | bytes 13107200 | tf_op jit(solution)/shard_map/concatenate | solution.py:342
  269.2 151.5 %shard_map.239 = (bf16[32,25,768]{2,1,0:T(8,128)(2,1)}, bf16[24,25,2048]{2,1,0:T(8,128)(2,1)}) custom-call(bf16[64,25,2048]{2,1,0:T(8,128)(2,1)} %pad_maximum_fusion.refs_0_), custom_call_target="tpu_custom_call" | custom-call | tf_op jit(solution)/shard_map/pallas_call | solution.py:400
  422.6 2.6 gather_fusion.1
  426.8 2.2 gather_fusion
  (81 shorter events, 26.8 us)
Async XLA Ops:
  31.9 106.6 %all-to-all-start = ((bf16[128,12,2048]{2,1,0:T(8,128)(2,1)}), bf16[128,12,2048]{2,1,0:T(8,128)(2,1)}, u32[]{:S(2)}, u32[]{:S(2)}) async-start(bf16[128,12,2048]{2,1,0:T(8,128)(2,1)} %bitcast.38), calls=%async_computation | async-start | bytes 16777216 | tf_op jit(solution)/shard_map/all_to_all | solution.py:391
  158.8 10.1 %collective-permute-start = (f32[768,1536]{1,0:T(8,128)}, f32[768,1536]{1,0:T(8,128)}, u32[]{:S(2)}, u32[]{:S(2)}) collective-permute-start(f32[768,1536]{1,0:T(8,128)} %fusion.9), channel_id=1, source_target_pairs={{0,1},{1,0},{2,3},{3,2},{4,5},{5,4},{6,7},{7,6},{8,9},{9,8},{10,11... | collective-permute-start | bytes 14155784 | tf_op jit(solution)/shard_map/ppermute | solution.py:273
  181.9 4.6 %collective-permute-start.1 = (bf16[768,1536]{1,0:T(8,128)(2,1)S(1)}, bf16[768,1536]{1,0:T(8,128)(2,1)S(1)}, u32[]{:S(2)}, u32[]{:S(2)}) collective-permute-start(bf16[768,1536]{1,0:T(8,128)(2,1)S(1)} %divide_convert_fusion.2), channel_id=1, source_target_pairs={{0,1},{1,0},{2,3},{3,2},{4,5},{5,4},{6,7},{7,6},{8,9},{9,8},{10,11... | collective-permute-start | bytes 7077896 | tf_op jit(solution)/shard_map/ppermute | solution.py:273
  182.1 6.4 %slice-start = ((s8[4718592]{0:T(1024)(128)(4,1)}), s8[4194304]{0:T(1024)(128)(4,1)S(1)}, s32[]{:S(2)}) async-start(s8[4718592]{0:T(1024)(128)(4,1)} %bitcast.36), calls=%async_computation.1 | async-start | bytes 8388608
  184.1 4.4 %slice-start.1 = ((s8[4718592]{0:T(1024)(128)(4,1)}), s8[524288]{0:T(1024)(128)(4,1)S(1)}, s32[]{:S(2)}) async-start(s8[4718592]{0:T(1024)(128)(4,1)} %bitcast.36), calls=%async_computation.2 | async-start | bytes 1048576
  188.5 12.4 %slice-start.2 = ((s8[6291456]{0:T(1024)(128)(4,1)}), s8[2097152]{0:T(1024)(128)(4,1)S(1)}, s32[]{:S(2)}) async-start(s8[6291456]{0:T(1024)(128)(4,1)} %bitcast.40), calls=%async_computation.3 | async-start | bytes 4194304
  191.8 10.8 %collective-permute-start.2 = (bf16[768,1536]{1,0:T(8,128)(2,1)}, bf16[768,1536]{1,0:T(8,128)(2,1)}, u32[]{:S(2)}, u32[]{:S(2)}) collective-permute-start(bf16[768,1536]{1,0:T(8,128)(2,1)} %add_convert_fusion.2), channel_id=1, source_target_pairs={{0,1},{1,0},{2,3},{3,2},{4,5},{5,4},{6,7},{7,6},{8,9},{9,8},{10,11... | collective-permute-start | bytes 7077896 | tf_op jit(solution)/shard_map/ppermute | solution.py:273
  192.1 8.8 %slice-start.3 = ((s8[6291456]{0:T(1024)(128)(4,1)}), s8[4194304]{0:T(1024)(128)(4,1)S(1)}, s32[]{:S(2)}) async-start(s8[6291456]{0:T(1024)(128)(4,1)} %bitcast.40), calls=%async_computation.4 | async-start | bytes 8388608
  209.5 6.8 %copy-start = (bf16[1536,2048]{1,0:T(8,128)(2,1)}, bf16[1536,2048]{1,0:T(8,128)(2,1)S(1)}, u32[]{:S(2)}) copy-start(bf16[1536,2048]{1,0:T(8,128)(2,1)S(1)} %fusion.2) | copy-start | bytes 18874372
  209.5 7.1 %copy-start.6 = (s32[24]{0:T(128)S(1)}, s32[24]{0:T(128)}, u32[]{:S(2)}) copy-start(s32[24]{0:T(128)} %param.21) | copy-start | bytes 292
  209.5 8.3 %copy-start.7 = (s32[32]{0:T(128)S(1)}, s32[32]{0:T(128)}, u32[]{:S(2)}) copy-start(s32[32]{0:T(128)} %param.20) | copy-start | bytes 388
  216.3 11.0 %collective-permute-start.3 = (f32[768,1536]{1,0:T(8,128)}, f32[768,1536]{1,0:T(8,128)}, u32[]{:S(2)}, u32[]{:S(2)}) collective-permute-start(f32[768,1536]{1,0:T(8,128)} %fusion.5), channel_id=1, source_target_pairs={{0,1},{1,0},{2,3},{3,2},{4,5},{5,4},{6,7},{7,6},{8,9},{9,8},{10,11... | collective-permute-start | bytes 14155784 | tf_op jit(solution)/shard_map/ppermute | solution.py:273
  227.2 9.6 %copy-start.4 = (f32[1344]{0:T(1024)S(1)}, f32[1344]{0:T(1024)}, u32[]{:S(2)}) copy-start(f32[1344]{0:T(1024)} %param.23) | copy-start | bytes 16132
  227.2 11.0 %copy-start.1 = (f32[128,768]{1,0:T(8,128)S(1)}, f32[128,768]{1,0:T(8,128)}, u32[]{:S(2)}) copy-start(f32[128,768]{1,0:T(8,128)} %param.30) | copy-start | bytes 1179652
  227.2 11.0 %copy-start.2 = (f32[128,768]{1,0:T(8,128)S(1)}, f32[128,768]{1,0:T(8,128)}, u32[]{:S(2)}) copy-start(f32[128,768]{1,0:T(8,128)} %param.28) | copy-start | bytes 1179652
  227.2 11.0 %copy-start.3 = (f32[128,768]{1,0:T(8,128)S(1)}, f32[128,768]{1,0:T(8,128)}, u32[]{:S(2)}) copy-start(f32[128,768]{1,0:T(8,128)} %param.27) | copy-start | bytes 1179652
  230.6 12.1 %collective-permute-start.4 = (bf16[768,1536]{1,0:T(8,128)(2,1)S(1)}, bf16[768,1536]{1,0:T(8,128)(2,1)}, u32[]{:S(2)}, u32[]{:S(2)}) collective-permute-start(bf16[768,1536]{1,0:T(8,128)(2,1)S(1)} %add_convert_fusion.1), channel_id=1, source_target_pairs={{0,1},{1,0},{2,3},{3,2},{4,5},{5,4},{6,7},{7,6},{8,9},{9,8},{10,11... | collective-permute-start | bytes 7077896 | tf_op jit(solution)/shard_map/ppermute | solution.py:273
  232.7 0.7 copy-start.8
  242.6 7.6 %slice-start.4 = ((s8[6291456]{0:T(1024)(128)(4,1)}), s8[4194304]{0:T(1024)(128)(4,1)S(1)}, s32[]{:S(2)}) async-start(s8[6291456]{0:T(1024)(128)(4,1)} %bitcast.42), calls=%async_computation.5 | async-start | bytes 8388608
  246.5 3.7 slice-start.5
  249.4 10.0 %collective-permute-start.5 = (bf16[768,1536]{1,0:T(8,128)(2,1)}, bf16[768,1536]{1,0:T(8,128)(2,1)S(1)}, u32[]{:S(2)}, u32[]{:S(2)}) collective-permute-start(bf16[768,1536]{1,0:T(8,128)(2,1)} %add_convert_fusion), channel_id=1, source_target_pairs={{0,1},{1,0},{2,3},{3,2},{4,5},{5,4},{6,7},{7,6},{8,9},{9,8},{10,11... | collective-permute-start | bytes 7077896 | tf_op jit(solution)/shard_map/ppermute | solution.py:273
  425.2 5.8 %copy-start.5 = (s32[56]{0:T(128)S(1)}, s32[56]{0:T(128)}, u32[]{:S(2)}) copy-start(s32[56]{0:T(128)} %param.22) | copy-start | bytes 676
